TPU v7x, 128 devices: a whole 4x4x4 slice. The times are simulated.
128 devices in a mesh: dp: 2 (over x_hi), pipe: 2 (over core), expert: 32 (over z, y, x_lo).
Axes of the slice: x: 4 (x_hi: 2, x_lo: 2; x = x_hi * 2 + x_lo), y: 4, z: 4, core: 2. Of those that a mesh axis runs over, the one named last changes fastest.
Arguments:
- inputs: bfloat16 [4, 2048, 1024], P(None, ('dp', 'expert')), may hold values from -6 to 6
- cotangent: bfloat16 [4, 2048, 1024], P(None, ('dp', 'expert')), may hold values from -0.29882812 to 0.29882812
- norm_gain: float32 [2, 1024], P('pipe'), may hold values from 0.5 to 1.5
- w_router: bfloat16 [2, 1024, 32], P('pipe'), may hold values from -0.1875 to 0.1875
- w_gate: bfloat16 [2, 32, 1024, 512], P('pipe', 'expert'), may hold values from -0.1875 to 0.1875
- w_up: bfloat16 [2, 32, 1024, 512], P('pipe', 'expert'), may hold values from -0.1875 to 0.1875
- w_down: bfloat16 [2, 32, 512, 1024], P('pipe', 'expert'), may hold values from -0.25 to 0.25
- routes: int32 [2, 4, 2048, 8], P('pipe', None, ('dp', 'expert')), may hold values from 0 to 31, all different within a row; in each aligned block of 32 rows (0 to 31, 32 to 63, ..., all dimensions but the last counted through in order) at most 10 rows name the same one
Outputs:
- grad_gate: bfloat16 [2, 32, 1024, 512], P('pipe', 'expert', 'dp')
- grad_up: bfloat16 [2, 32, 1024, 512], P('pipe', 'expert', 'dp')
- grad_down: bfloat16 [2, 32, 512, 1024], P('pipe', 'expert', None, 'dp')
- grad_router: float32 [2, 1024, 32], P('pipe')
- grad_gain: float32 [2, 1024], P('pipe')
Inputs may be any that keep to these rules, and one draw needn't show every extreme that they name: `routes`: the experts of a token differ. Among the 32 tokens of one device in one layer and micro-batch, no expert is picked by more than 10 tokens, and some expert is picked by exactly 10 in some of them.
All inputs are finite; a program needn't handle non-finite values.
Results may differ from a plain program's by a relative error of at most 0.012.
Values may be sent and summed in bfloat16 or wider, within the bound.
No kernel may reach another device: no remote copies, remote signals or barrier semaphores. Data moves between devices by JAX's collectives and lax.ppermute only.
A program may use at most 128 MiB of HBM per device.

v0:
```python
import jax
import jax.numpy as jnp
import numpy as np
from jax import lax
from jax.experimental import pallas as pl
from jax.experimental.pallas import tpu as pltpu
from jax.sharding import PartitionSpec as P


EPS = 1e-05
BF = jnp.bfloat16
F32 = jnp.float32

ROWS = 32
CAP = 10
HALF = 2
TOK = ROWS * HALF
EXP = 32
USED = CAP * HALF
LANE = 128
LINES = 8
PACK = EXP * LINES
REST = USED - 2 * LINES
ALL = EXP * USED
PARTS = ((0, PACK), (PACK, ALL - PACK))


def dot(a, b):
    return lax.dot_general(a, b, (((1,), (0,)), ((), ())), preferred_element_type=F32)


def dot_t0(a, b):
    return lax.dot_general(a, b, (((0,), (0,)), ((), ())), preferred_element_type=F32)


def dot_t1(a, b):
    return lax.dot_general(a, b, (((1,), (1,)), ((), ())), preferred_element_type=F32)


def split2(v):
    hi = v.astype(BF)
    return hi, (v - hi.astype(F32)).astype(BF)


def split3(v):
    hi = v.astype(BF)
    rest = v - hi.astype(F32)
    mid = rest.astype(BF)
    return hi, mid, (rest - mid.astype(F32)).astype(BF)


def flags(test):
    return jnp.where(test, 1.0, 0.0).astype(BF)


def count(shape, axis):
    return lax.broadcasted_iota(jnp.int32, shape, axis).astype(F32)


def over(v, by):
    whole = jnp.floor((v + 0.5) * (1.0 / by))
    return whole, v - by * whole


def row_place(first, shape, axis):
    s = count(shape, axis) + first
    group, inner = over(s, PACK)
    source, line = over(inner, LINES)
    source_rest, line_rest = over(inner, REST)
    rest = group >= 2
    return jnp.where(rest, source_rest, source), jnp.where(rest, line_rest, line) + LINES * group


def line_place(shape, axis):
    return over(count(shape, axis), LINES)


def column_place(shape, axis):
    group, inner = over(count(shape, axis), PACK)
    partner, line = over(inner, LINES)
    slot = jnp.where(group >= 3, jnp.where(line >= REST, line + (2 * LINES - REST), -9.0), line + LINES * group)
    return partner, slot


def expand_of():
    shape = (EXP, 4 * PACK)
    return flags(column_place(shape, 1)[0] == count(shape, 0))


def expand_t_of():
    shape = (4 * PACK, EXP)
    return flags(column_place(shape, 0)[0] == count(shape, 1))


def slots_of(picks, expand):
    columns = lax.broadcasted_iota(jnp.int32, (TOK, EXP), 1)
    mask = jnp.zeros((TOK, EXP), F32)
    for k in range(picks.shape[1]):
        mask = mask + jnp.where(picks[:, k : k + 1] == columns, 1.0, 0.0)
    row = lax.broadcasted_iota(jnp.int32, (TOK, TOK), 0)
    column = lax.broadcasted_iota(jnp.int32, (TOK, TOK), 1)
    earlier = flags((column < row) & ((row < ROWS) | (column >= ROWS)))
    start = jnp.where(lax.broadcasted_iota(jnp.int32, (TOK, EXP), 0) < ROWS, 0.0, 1.0 * CAP)
    slot = mask * (dot(earlier, mask.astype(BF)) + start + 1.0) - 1.0
    table = dot(slot.astype(BF), expand) == column_place((1, 4 * PACK), 1)[1]
    return mask, table, slot


def norm(tokens, gain):
    values = tokens.astype(F32)
    scale = lax.rsqrt(jnp.mean(values * values, axis=-1, keepdims=True) + EPS)
    return (values * scale * gain).astype(BF), scale, values


def mix(normed, router, mask):
    logits = dot_t1(normed, router)
    expo = jnp.where(mask > 0.0, jnp.exp(jnp.where(mask > 0.0, logits, 0.0)), 0.0)
    return expo / jnp.sum(expo, axis=-1, keepdims=True)


def weighted(table, parts, expand):
    return [jnp.where(table, dot(v, expand), 0.0).astype(BF) for v in parts]


def to_packed(picked, rows, out, done, first=0):
    half = rows.shape[1] // 2
    width = 2 * half
    for i in range(2):
        columns = slice(i * PACK, (i + 1) * PACK)
        out[:, first + i * width : first + (i + 1) * width] = sum(dot_t0(v[:, columns], rows) for v in picked).astype(BF)
        done(i)
    low, high = slice(2 * PACK, 3 * PACK), slice(3 * PACK, 4 * PACK)
    last = sum(dot_t0(v[:, low], rows[:, :half]) + dot_t0(v[:, high], rows[:, half:]) for v in picked)
    out[:, first + 2 * width : first + 2 * width + half] = last.astype(BF)
    done(2)


def from_packed(picked, packed, width):
    half = width // 2
    rest = packed[:, 2 * width : 2 * width + half]
    total = sum(
        dot(v[:, :PACK], packed[:, :width]) + dot(v[:, PACK : 2 * PACK], packed[:, width : 2 * width]) for v in picked
    )
    low = sum(dot(v[:, 2 * PACK : 3 * PACK], rest) for v in picked)
    high = sum(dot(v[:, 3 * PACK :], rest) for v in picked)
    return total + jnp.concatenate([low, high], axis=1)


def rest_tables():
    shape = (EXP * REST, PACK)
    source, line = over(count(shape, 0), REST)
    place, at = line_place(shape, 1)
    return flags((source == place) & (line == at)), flags((source == place) & (line + REST == at))


def unpack(packed, first, width, out, piece):
    if piece == 0:
        out[0:PACK, :] = packed[:, first : first + width]
        return
    half = width // 2
    out[PACK : 2 * PACK, :] = packed[:, first + width : first + 2 * width]
    rest = packed[:, first + 2 * width : first + 2 * width + half]
    low, high = rest_tables()
    out[2 * PACK :, :half] = dot(low, rest).astype(BF)
    out[2 * PACK :, half:] = dot(high, rest).astype(BF)


def pack(rows, out, piece):
    width = rows.shape[1]
    if piece == 0:
        out[:, :width] = rows
        return
    half = width // 2
    out[:, width : 2 * width] = rows[:PACK, :]
    low, high = rest_tables()
    rest = dot_t0(low, rows[PACK:, :half]) + dot_t0(high, rows[PACK:, half:])
    out[:, 2 * width : 2 * width + half] = rest.astype(BF)


def line_table(first, number, test):
    shape = (number, PACK)
    source, line = line_place(shape, 1)
    return flags((row_place(first, shape, 0)[0] == source) & test(line))


def slot_lanes(first, number):
    shape = (number, LANE)
    return row_place(first, shape, 0)[1] == count(shape, 1)


def column_of(small, first, number, test):
    wide = dot(line_table(first, number, test), small)
    return jnp.sum(jnp.where(slot_lanes(first, number), wide, 0.0), axis=1, keepdims=True)


def small_lines(masked):
    shape = (3 * PACK, LANE)
    place = flags(column_place(shape, 0)[1] == count(shape, 1))
    shape = (PACK, 3 * PACK)
    source, line = line_place(shape, 0)
    same = source == column_place(shape, 1)[0]
    total = None
    for i, v in enumerate(masked):
        row = jnp.sum(v[:, : 3 * PACK].astype(F32), axis=0, keepdims=True)
        part = dot(jnp.where(same & (line == i), row, 0.0).astype(BF), place)
        total = part if total is None else total + part
    return total.astype(BF)


def cost(flops, arrays):
    size = sum(int(np.prod(a.shape)) * jnp.dtype(a.dtype).itemsize for a in arrays)
    return pl.CostEstimate(flops=flops, bytes_accessed=size, transcendentals=0)


def cuts(sizes):
    return [(sum(sizes[:i]), size) for i, size in enumerate(sizes)]


def view(ref, axis, cut):
    return ref.at[(slice(None),) * axis + (pl.ds(*cut),)]


class Load:
    def __init__(self, array, sizes=None, axis=0, first=0, width=None):
        self.array, self.axis, self.first = array, axis, first
        self.width = width or array.shape[-1]
        self.shape = tuple(array.shape[:-1]) + (self.width,)
        self.dtype = array.dtype
        self.cuts = cuts(sizes or (self.shape[axis],))
        self.other = None

    def copies(self, src, dst, sem, at):
        if self.width != self.array.shape[-1]:
            src = view(src, len(self.shape) - 1, (self.first, self.width))
        return [
            pltpu.make_async_copy(view(src, self.axis, cut), view(dst, self.axis, cut), sem.at[i])
            for i, cut in enumerate(self.cuts)
        ]


class Tokens(Load):
    def __init__(self, array):
        super().__init__(array)
        self.shape = (TOK, array.shape[1])
        self.cuts = [(0, TOK)]

    def copies(self, src, dst, sem, at):
        return [pltpu.make_async_copy(src.at[pl.ds(pl.multiple_of(at[0] * TOK, TOK), TOK)], dst, sem.at[0])]


class Either(Load):
    def __init__(self, array, other, sizes):
        super().__init__(array, sizes)
        self.other = other


class Moves:
    def __init__(self, loads, stores):
        self.loads, self.stores, self.taken = loads, stores, set()

    def start(self, order):
        for i, piece in order or [(i, p) for i, load in enumerate(self.loads) for p in range(len(load))]:
            self.loads[i][piece].start()

    def need(self, *names):
        for name in names:
            i, piece = name if isinstance(name, tuple) else (name, None)
            for p in range(len(self.loads[i])) if piece is None else [piece]:
                if (i, p) not in self.taken:
                    self.taken.add((i, p))
                    self.loads[i][p].wait()

    def flush(self, piece, *outs):
        for j in outs:
            self.stores[j][piece].start()

    def end(self):
        self.need(*range(len(self.loads)))
        for store in self.stores:
            for copy in store:
                copy.wait()


def call(body, outs, args, flops, at=None, scratch=(), order=None):
    args = [v if isinstance(v, Load) else Load(v) for v in args]
    others = [v.other for v in args if v.other is not None]
    out_shape = [jax.ShapeDtypeStruct(out[0], out[1]) for out in outs]
    ways = [(out[2], cuts(out[3])) if len(out) > 2 else (0, [(0, out[0][0])]) for out in outs]
    scalars = [] if at is None else [at]
    n, m = len(args), len(outs)

    def kernel(*refs):
        where = refs[0] if scalars else None
        refs = refs[len(scalars) :]
        ins, twins, refs = refs[:n], refs[n : n + len(others)], refs[n + len(others) :]
        results, held, refs = refs[:m], refs[m : m + n], refs[m + n :]
        made, load_sems, store_sems = refs[:m], refs[m : m + n], refs[m + n : m + n + m]
        own = refs[m + n + m :]
        loads = [v.copies(src, dst, sem, where) for v, src, dst, sem in zip(args, ins, held, load_sems)]
        stores = [
            [
                pltpu.make_async_copy(view(made[j], axis, cut), view(results[j], axis, cut), store_sems[j].at[i])
                for i, cut in enumerate(pieces)
            ]
            for j, (axis, pieces) in enumerate(ways)
        ]
        moves = Moves(loads, stores)
        if others:
            for pick, sources in enumerate((ins, twins)):

                @pl.when(where[0] == pick)
                def _():
                    picked = [v.copies(*way, where) for v, *way in zip(args, sources, held, load_sems)]
                    for piece in range(len(args[0].cuts)):
                        for copies in picked:
                            copies[piece].start()

        else:
            moves.start(order)
        body(moves, where, held, made, *own)
        moves.end()

    hbm = pl.BlockSpec(memory_space=pl.ANY)
    return pl.pallas_call(
        kernel,
        out_shape=out_shape,
        in_specs=[pl.BlockSpec(memory_space=pltpu.SMEM)] * len(scalars) + [hbm] * (n + len(others)),
        out_specs=[hbm] * m,
        scratch_shapes=[pltpu.VMEM(v.shape, v.dtype) for v in args]
        + [pltpu.VMEM(s.shape, s.dtype) for s in out_shape]
        + [pltpu.SemaphoreType.DMA((len(v.cuts),)) for v in args]
        + [pltpu.SemaphoreType.DMA((len(pieces),)) for axis, pieces in ways]
        + list(scratch),
        cost_estimate=cost(flops, [v.array for v in args] + out_shape),
        compiler_params=pltpu.CompilerParams(vmem_limit_bytes=63 << 20),
    )(*scalars, *[v.array for v in args], *others)


def start_body(moves, at, ins, outs):
    inputs, cotangent, picks0, picks1, gain_own, gain_other, router_own, router_other = ins
    send, weights, tokens, grad, gains, routers = outs
    mine = at[0] == 0
    expand = expand_of()
    moves.need(2, 3)
    mask, table0, _ = slots_of(picks0[...], expand)
    table1 = slots_of(picks1[...], expand)[1]
    moves.need(0, 1, 4, 5)
    own, other = gain_own[...], gain_other[...]
    gain0 = jnp.where(mine, own, other)
    gains[0:1, :] = gain0
    gains[1:2, :] = jnp.where(mine, other, own)
    token, cot = inputs[...], cotangent[...]
    normed, _, _ = norm(token, gain0)
    to_packed([flags(table0)], normed, send, lambda i: moves.flush(i, 0))
    to_packed([flags(table1)], cot, send, lambda i: moves.flush(3 + i, 0), send.shape[1] // 2)
    tokens[...] = token
    grad[...] = cot
    moves.need(6, 7)
    own, other = router_own[...], router_other[...]
    router0 = jnp.where(mine, own, other)
    routers[0:EXP, :] = router0
    routers[EXP:, :] = jnp.where(mine, other, own)
    weights[...] = mix(normed, router0, mask)
    moves.flush(0, 1, 2, 3, 4, 5)


def forward_body(moves, at, ins, outs, rows):
    x, wg, wu, wd = ins
    (out,) = outs
    width = rows.shape[1]
    for i, (first, number) in enumerate(PARTS):
        part = pl.ds(first, number)
        moves.need(*[(0, 0)] if i == 0 else [(0, 1), (0, 2)])
        unpack(x, 0, width, rows, i)
        moves.need(1)
        gate = dot(rows[part, :], wg[...])
        moves.need(2)
        up = dot(rows[part, :], wu[...])
        hidden = (jax.nn.silu(gate) * up).astype(BF)
        moves.need(3)
        pack(dot(hidden, wd[...]).astype(BF), out, i)
        for piece in [0] if i == 0 else [1, 2]:
            moves.flush(piece, 0)


def residual_body(moves, at, ins, outs):
    x, wg, wu = ins
    fa, fb, hid, rows, grad = outs
    width = rows.shape[1]
    for i, (first, number) in enumerate(PARTS):
        part = pl.ds(first, number)
        moves.need(0, 1)
        unpack(x, 0, width, rows, i)
        unpack(x, x.shape[1] // 2, width, grad, i)
        gate = dot(rows[part, :], wg[...])
        moves.need(2)
        up = dot(rows[part, :], wu[...])
        sig = jax.nn.sigmoid(gate)
        act = gate * sig
        hid[part, :] = (act * up).astype(BF)
        fb[part, :] = act
        fa[part, :] = up * sig * (1.0 + gate * (1.0 - sig))
        moves.flush(i, 0, 1, 2, 3, 4)


def expert1_body(moves, at, ins, outs):
    x, g, wg, wu, wd = ins
    send, rows, scaled_out, gate_out, up_out, hid = outs
    width = rows.shape[1]
    moves.need(0)
    small = x[:, x.shape[1] - LANE :]
    told = [jnp.zeros((PACK, LANE), F32) for _ in range(3)]
    for i, (first, number) in enumerate(PARTS):
        part = pl.ds(first, number)
        unpack(x, 0, width, rows, i)
        moves.need(2)
        gate = dot(rows[part, :], wg[...])
        moves.need(3)
        up = dot(rows[part, :], wu[...])
        sig = jax.nn.sigmoid(gate)
        act = gate * sig
        hidden = (act * up).astype(BF)
        hid[part, :] = hidden
        moves.need(4)
        out = dot(hidden, wd[...]).astype(BF)
        weight = column_of(small, first, number, lambda line: line < 2)
        moves.need((1, i))
        grad = g[part, :].astype(F32)
        weight_grad = jnp.sum(grad * out.astype(F32), axis=1, keepdims=True)
        scaled = (weight * grad).astype(BF)
        scaled_out[part, :] = scaled
        grad_hidden = dot_t1(scaled, wd[...])
        gate_back = (grad_hidden * (up * sig * (1.0 + gate * (1.0 - sig)))).astype(BF)
        up_back = (grad_hidden * act).astype(BF)
        gate_out[part, :] = gate_back
        up_out[part, :] = up_back
        pack((dot_t1(gate_back, wg[...]) + dot_t1(up_back, wu[...])).astype(BF), send, i)
        placed = jnp.where(slot_lanes(first, number), weight_grad, 0.0)
        for k, v in enumerate(split3(placed)):
            told[k] = told[k] + dot_t0(line_table(first, number, lambda line: line == k), v)
        moves.flush(i, 1, 2, 3, 4, 5)
        if i == 0:
            moves.flush(0, 0)
    send[:, send.shape[1] - LANE :] = (told[0] + told[1] + told[2]).astype(BF)
    moves.flush(1, 0)
    moves.flush(2, 0)


def blocks_of(gb, ub, x, sc, hid, group, which, out):
    half, quarter = x.shape[1] // 2, x.shape[1] // 4
    rows = x[:, pl.ds(pl.multiple_of(group * half + which * quarter, quarter), quarter)]
    gate = dot_t0(rows, gb[...])
    up = dot_t0(rows, ub[...])
    out[0:quarter, :] = gate.astype(BF)
    out[quarter : 2 * quarter, :] = up.astype(BF)
    low = hid[:, pl.ds(pl.multiple_of(which * quarter, quarter), quarter)]
    wide = sc[:, pl.ds(pl.multiple_of(group * half, half), half)]
    out[2 * quarter :, :] = dot_t0(low, wide).astype(BF)
    return gate, up


def four_blocks(at):
    return [(group, which) for group in (1 - at[1], at[1]) for which in (1 - at[0], at[0])]


def grads1_body(moves, at, ins, outs):
    gb, ub, x, sc, hid = ins
    moves.need(0, 1, 2, 3, 4)
    for j, (group, which) in enumerate(four_blocks(at)):
        blocks_of(gb, ub, x, sc, hid, group, which, outs[j])
        moves.flush(0, j)


def backward0_body(moves, at, ins, outs, rows, gb, ub, total):
    sc, fa, fb, wd, x, hid, wg, wu, x1, layer_gains, gains = ins
    mine, theirs = outs[4:]
    width = rows.shape[1]
    moves.need(3)
    for i, (first, number) in enumerate(PARTS):
        part = pl.ds(first, number)
        moves.need(*[(0, 0)] if i == 0 else [(0, 1), (0, 2)])
        moves.need((1, i), (2, i))
        unpack(sc, 0, width, rows, i)
        grad_hidden = dot_t1(rows[part, :], wd[...])
        gb[part, :] = (grad_hidden * fa[part, :]).astype(BF)
        ub[part, :] = (grad_hidden * fb[part, :]).astype(BF)
    moves.need(4, 5, 6, 7)
    half, quarter = width // 2, width // 4
    shape = (quarter, quarter)
    same = lax.broadcasted_iota(jnp.int32, shape, 0) == lax.broadcasted_iota(jnp.int32, shape, 1)
    for j, (group, which) in enumerate(four_blocks(at)):
        gate, up = blocks_of(gb, ub, x, rows, hid, group, which, outs[j])
        moves.flush(0, j)
        place = pl.ds(pl.multiple_of(group * half + which * quarter, quarter), quarter)
        column = jnp.sum(gate * wg[place, :].astype(F32) + up * wu[place, :].astype(F32), axis=1, keepdims=True)
        total[1:2, place] = jnp.sum(jnp.where(same, column, 0.0), axis=0, keepdims=True)
    moves.need(8, 9, 10)
    small = sc[:, sc.shape[1] - LANE :]
    for line, array, index in ((0, x, 0), (2, x1, 1)):
        column = column_of(small, 0, ALL, lambda at_line: at_line == index)
        wide = jnp.broadcast_to(column, (ALL, LANE)).astype(BF)
        total[line : line + 1, :] = dot_t0(wide, array[...])[0:1, :]
    gain0 = total[1:2, :] / layer_gains[0:1, :] + gains[1:2, :]
    gain1 = gains[0:1, :]
    first = at[0] == 0
    column0, column1 = total[0:1, :], total[2:3, :]
    mine[0:1, :] = jnp.where(first, column0, column1)
    mine[1:2, :] = jnp.where(first, gain0, gain1)
    theirs[0:1, :] = jnp.where(first, column1, column0)
    theirs[1:2, :] = jnp.where(first, gain1, gain0)
    moves.flush(0, 4, 5)


def told_body(moves, at, ins, outs):
    own, other = ins
    (out,) = outs
    moves.need(0, 1)
    group, lines, lane = out.shape
    both = own[...] + other[...]
    for v in range(2):
        for j in range(lines // 2):
            piece = both[v : v + 1, j * lane : (j + 1) * lane]
            out[:, v * (lines // 2) + j, :] = jnp.broadcast_to(piece, (group, lane))
    moves.flush(0, 0)


def heard_body(moves, at, ins, outs):
    (heard,) = ins
    router, gain = outs
    moves.need(0)
    _, lines, lane = heard.shape
    for j in range(lines // 2):
        column = slice(j * lane, (j + 1) * lane)
        router[:, column] = heard[0:EXP, j, :] + heard[EXP:, j, :]
        gain[:, column] = jnp.sum(heard[:, lines // 2 + j, :], axis=0, keepdims=True)
    moves.flush(0, 0, 1)


def finish_body(moves, at, ins, outs):
    low, high, low_got, high_got = ins
    quarter = low.shape[0] // 3
    for i, out in enumerate(outs):
        moves.need(*[(k, i) for k in range(4)])
        rows = slice(i * quarter, (i + 1) * quarter)
        out[0:quarter, :] = (low[rows, :].astype(F32) + low_got[rows, :].astype(F32)).astype(BF)
        out[quarter:, :] = (high[rows, :].astype(F32) + high_got[rows, :].astype(F32)).astype(BF)
        moves.flush(0, i)


def middle_body(moves, at, ins, outs):
    tokens, picks0, weights0, returned, picks1, gains, routers = ins
    mixed_out, send, weights1 = outs
    width = tokens.shape[1]
    expand = expand_of()
    moves.need(1, 2, 4)
    _, table0, _ = slots_of(picks0[...], expand)
    parts = weighted(table0, split2(weights0[...]), expand)
    mask1, table1, _ = slots_of(picks1[...], expand)
    moves.need(0, 3, 5, 6)
    mixed = (tokens[...].astype(F32) + from_packed(parts, returned, width)).astype(BF)
    mixed_out[...] = mixed
    normed, _, _ = norm(mixed, gains[1:2, :])
    weights = mix(normed, routers[EXP:, :], mask1)
    weights1[...] = weights
    send[:, send.shape[1] - LANE :] = small_lines(weighted(table1, split2(weights), expand))
    to_packed([flags(table1)], normed, send, lambda i: moves.flush(i, 1))
    moves.flush(0, 0, 2)


def turn_body(moves, at, ins, outs):
    tokens1, picks1, weights1, returned1, grad, tokens0, picks0, weights0, returned0, gains, routers = ins
    send, gains_out = outs
    width = tokens1.shape[1]
    half = width // 2
    expand = expand_of()
    moves.need(0, 1, 2, 4, 5, 6, 7, 9, 10)
    gain0, gain1 = gains[0:1, :], gains[1:2, :]
    _, table1, slot1 = slots_of(picks1[...], expand)
    _, table0, _ = slots_of(picks0[...], expand)
    w0, w1 = weights0[...], weights1[...]
    parts0 = weighted(table0, split2(w0), expand)
    _, scale0, values0 = norm(tokens0[...], gain0)
    _, scale1, values1 = norm(tokens1[...], gain1)
    moves.need(3)
    expert_part = from_packed([flags(table1)], returned1, width)
    shape = (PACK, EXP)
    source, line = line_place(shape, 0)
    told = dot_t0(returned1[:, returned1.shape[1] - LANE :], flags((source == count(shape, 1)) & (line < 3)))
    wg1 = jnp.zeros((TOK, EXP), F32)
    for i in range(USED):
        wg1 = jnp.where(slot1 == i, told[i : i + 1, :], wg1)
    lg1 = (w1 * (wg1 - jnp.sum(w1 * wg1, axis=-1, keepdims=True))).astype(BF)
    normed_grad1 = dot(lg1, routers[EXP:, :]) + expert_part
    gains_out[0:1, :] = jnp.sum(normed_grad1 * values1 * scale1, axis=0, keepdims=True)
    q = normed_grad1 * gain1
    grad_f = grad[...].astype(F32)
    g0 = (
        grad_f + scale1 * q - scale1 * scale1 * scale1 * values1 * jnp.mean(q * values1, axis=-1, keepdims=True)
    ).astype(BF)
    moves.need(8)
    rest = returned0[:, 2 * width : 2 * width + half]
    met = jnp.concatenate(
        [
            dot_t1(g0, returned0[:, :width]),
            dot_t1(g0, returned0[:, width : 2 * width]),
            dot_t1(g0[:, :half], rest),
            dot_t1(g0[:, half:], rest),
        ],
        axis=1,
    )
    met = jnp.where(table0, met, 0.0)
    expand_t = expand_t_of()
    wg0 = jnp.zeros((TOK, EXP), F32)
    for part in split3(met):
        wg0 = wg0 + dot(part, expand_t)
    lg0 = (w0 * (wg0 - jnp.sum(w0 * wg0, axis=-1, keepdims=True))).astype(BF)
    gains_out[1:2, :] = jnp.sum(dot(lg0, routers[0:EXP, :]) * values0 * scale0, axis=0, keepdims=True)
    lines = [weighted(table0, [lg0], expand)[0], weighted(table1, [lg1], expand)[0]]
    send[:, send.shape[1] - LANE :] = small_lines(lines)
    to_packed(parts0, g0, send, lambda i: moves.flush(i, 0))
    moves.flush(0, 1)


def exchanged(rows):
    return lax.all_to_all(rows, "expert", split_axis=0, concat_axis=0, tiled=True)


def swapped(value):
    return lax.ppermute(value, "pipe", [(0, 1), (1, 0)])


def shards(inputs, cotangent, norm_gain, w_router, w_gate, w_up, w_down, routes):
    pipe = lax.axis_index("pipe")
    data = lax.axis_index("dp")
    at = jnp.stack([pipe, data]).astype(jnp.int32)
    width = inputs.shape[-1]
    inner = w_gate.shape[-1]
    half, quarter = width // 2, width // 4
    first = pipe == 0
    flops = ALL * width * inner

    def part_of(v, which):
        return lax.dynamic_slice_in_dim(v, which * HALF, HALF, 0).reshape(TOK, -1)

    def both(own, other):
        return jnp.where(first, own, other), jnp.where(first, other, own)

    picks0, picks1 = both(part_of(routes[0], pipe), swapped(part_of(routes[0], 1 - pipe)))
    router = w_router[0].T
    packed = 2 * width + half
    pieces = (width, width, half)
    with_small = (width, width, half + LANE)
    part_rows = [number for first, number in PARTS]
    rows_shape = ((ALL, width), BF, 0, part_rows)
    inner_shape = ((ALL, inner), BF, 0, part_rows)
    wide_shape = ((ALL, inner), F32, 0, part_rows)
    small_shape = ((PACK, packed + LANE), BF, 1, with_small)
    few = ((TOK, width), BF)
    send0, weights0, tokens0, grad1, gains, routers = call(
        start_body,
        [((PACK, 2 * packed), BF, 1, pieces * 2), ((TOK, EXP), F32), few, few, ((2, width), F32), ((2 * EXP, width), BF)],
        [
            Tokens(inputs.reshape(-1, width)),
            Tokens(cotangent.reshape(-1, width)),
            picks0,
            picks1,
            norm_gain,
            swapped(norm_gain),
            router,
            swapped(router),
        ],
        400_000_000,
        at,
    )
    arrived = exchanged(send0)
    mats = [both(w[0, 0], swapped(w[0, 0])) for w in (w_gate, w_up, w_down)]
    (gate0, gate1), (up0, up1), (down0, down1) = lax.optimization_barrier(mats)

    (out0,) = call(
        forward_body,
        [((PACK, packed), BF, 1, pieces)],
        [Load(arrived, pieces, 1, 0, packed), gate0, up0, down0],
        6 * flops,
        scratch=[pltpu.VMEM((ALL, width), BF)],
        order=[(0, 0), (1, 0), (2, 0), (3, 0), (0, 1), (0, 2)],
    )
    returned0 = exchanged(out0)
    fa0, fb0, hidden0, recv0, grad_rows = call(
        residual_body, [wide_shape, wide_shape, inner_shape, rows_shape, rows_shape], [arrived, gate0, up0], 4 * flops
    )
    returned0, grad_rows = lax.optimization_barrier((returned0, grad_rows))

    tokens1, send1, weights1 = call(
        middle_body,
        [few, small_shape, ((TOK, EXP), F32)],
        [tokens0, picks0, weights0, returned0, picks1, gains, routers],
        600_000_000,
    )
    arrived1 = exchanged(send1)
    send_b, rows1, scaled1, gate_back1, up_back1, hidden1 = call(
        expert1_body,
        [small_shape, rows_shape, rows_shape, inner_shape, inner_shape, inner_shape],
        [arrived1, Load(grad_rows, part_rows), gate1, up1, down1],
        12 * flops,
        order=[(0, 0), (2, 0), (3, 0), (4, 0), (1, 0), (1, 1)],
    )
    returned1 = exchanged(send_b)

    block = ((3 * quarter, half), BF)

    def to_owner(paired, owner):
        return [
            lax.ppermute(paired, ("dp", "pipe"), [(2 * d + p, 2 * (1 - d) + owner) for d in range(2)]) for p in range(2)
        ]

    def paired_of(kept, swap):
        return (kept.astype(F32) + swap.astype(F32)).astype(BF)

    args1 = [gate_back1, up_back1, rows1, scaled1, hidden1]
    sent, kept, sent_near, kept_near = call(grads1_body, [block] * 4, args1, 6 * flops, at)
    paired1 = paired_of(kept, swapped(sent))
    got1 = to_owner(paired1, 1)

    send2, token_gains = call(
        turn_body,
        [small_shape, ((2, width), F32)],
        [tokens1, picks1, weights1, returned1, grad1, tokens0, picks0, weights0, returned0, gains, routers],
        900_000_000,
    )
    recv2 = exchanged(send2)
    sum1 = paired_of(kept_near, swapped(sent_near))
    low1 = lax.ppermute(sum1, "pipe", [(0, 1)])
    recv2, low1, sum1, got1 = lax.optimization_barrier((recv2, low1, sum1, got1))

    few_rows = ((2, width), F32)
    sent, kept, sent_near, kept_near, small, others = call(
        backward0_body,
        [block] * 4 + [few_rows] * 2,
        [Load(recv2, with_small, 1), Load(fa0, part_rows), Load(fb0, part_rows), down0, recv0, hidden0]
        + [gate0, up0, rows1, gains, token_gains],
        9 * flops,
        at,
        [pltpu.VMEM((ALL, width), BF), pltpu.VMEM((ALL, inner), BF), pltpu.VMEM((ALL, inner), BF)]
        + [pltpu.VMEM((8, width), F32)],
        order=[(3, 0), (0, 0), (1, 0), (2, 0), (0, 1), (0, 2), (1, 1), (2, 1)] + [(i, 0) for i in range(4, 11)],
    )
    paired0 = paired_of(kept, swapped(sent))
    got0 = to_owner(paired0, 0)
    told = call(told_body, [((2 * EXP, 2 * width // LANE, LANE), F32)], [small, swapped(others)], 1000)[0]
    heard = lax.all_to_all(told, ("dp", "expert"), split_axis=0, concat_axis=0, tiled=True)
    sum0 = paired_of(kept_near, swapped(sent_near))
    high0 = lax.ppermute(sum0, "pipe", [(1, 0)])
    router_sum, gain_sum = call(heard_body, [((EXP, width), F32), ((1, width), F32)], [heard], 1000)
    thirds = (quarter,) * 3
    final = ((2 * quarter, half), BF)
    outs = call(
        finish_body,
        [final] * 3,
        [
            Either(sum0, low1, thirds),
            Either(high0, sum1, thirds),
            Either(got0[0], got1[0], thirds),
            Either(got0[1], got1[1], thirds),
        ],
        1000,
        at,
    )
    return (
        outs[0][None, None],
        outs[1][None, None],
        outs[2][None, None],
        router_sum.T[None],
        gain_sum,
    )


def solution(mesh):
    in_specs = (
        P(None, ("dp", "expert"), None),
        P(None, ("dp", "expert"), None),
        P("pipe", None),
        P("pipe", None, None),
        P("pipe", "expert", None, None),
        P("pipe", "expert", None, None),
        P("pipe", "expert", None, None),
        P("pipe", None, ("dp", "expert"), None),
    )
    out_specs = (
        P("pipe", "expert", "dp", None),
        P("pipe", "expert", "dp", None),
        P("pipe", "expert", None, "dp"),
        P("pipe", None, None),
        P("pipe", None),
    )

    return jax.shard_map(shards, mesh=mesh, in_specs=in_specs, out_specs=out_specs, check_vma=False)
```

profile of v0, /device:TPU:0, one launch (start us, length us, event | category | flops | bytes accessed | tf_op | source)
XLA Modules:
  0.0 250.4 jit_solution(6933834958121108356)
XLA Ops:
  4.2 4.4 %shard_map.119 = (bf16[256,5120]{1,0:T(8,128)(2,1)}, f32[64,32]{1,0:T(8,128)}, bf16[64,1024]{1,0:T(8,128)(2,1)}, bf16[64,1024]{1,0:T(8,128)(2,1)}, f32[2,1024]{1,0:T(2,128)}, /*index=5*/bf16[64,1024]{1,0:T(8,128)(2,1)}) custom-call(s32[2]{0:T(128)} %pad_add_fusion.refs_0_, bf16[128,1024]{1,0:T(8,128)(2,1)} %bitcast.49, bf16[128,1024]{1,0:T(8,128)(2,1)} %bitcast.50, ...), custom_call_target="tpu_custom_call" | custom-call | flops 400000000 | bytes 3698688 | tf_op jit(solution)/shard_map/pallas_call | solution.py:324
  8.6 9.8 %all-to-all-start = ((bf16[32,8,5120]{2,1,0:T(8,128)(2,1)}), bf16[32,8,5120]{2,1,0:T(8,128)(2,1)}, u32[]{:S(2)}, u32[]{:S(2)}) async-start(bf16[32,8,5120]{2,1,0:T(8,128)(2,1)} %bitcast.36), calls=%async_computation | async-start | bytes 5242880 | tf_op jit(solution)/shard_map/all_to_all | solution.py:625
  19.1 2.0 collective-permute-done.5
  21.1 1.5 broadcast_select_fusion
  22.7 1.5 broadcast_select_fusion.2
  24.2 1.5 broadcast_select_fusion.4
  25.6 29.7 %all-to-all-done = bf16[32,8,5120]{2,1,0:T(8,128)(2,1)} async-done(((bf16[32,8,5120]{2,1,0:T(8,128)(2,1)}), bf16[32,8,5120]{2,1,0:T(8,128)(2,1)}, u32[]{:S(2)}, u32[]{:S(2)}) %all-to-all-start) | async-done | bytes 2621472 | tf_op jit(solution)/shard_map/all_to_all | solution.py:625
  55.4 5.7 %shard_map.120 = bf16[256,2560]{1,0:T(8,128)(2,1)} custom-call(bf16[256,5120]{1,0:T(8,128)(2,1)} %bitcast.10.refs_0_, bf16[1024,512]{1,0:T(8,128)(2,1)} %get-tuple-element.58.refs_1_.refs_7_, bf16[1024,512]{1,0:T(8,128)(2,1)} %get-tuple-element.59.refs_2_.refs_8_, bf16[512,1024]{1,0:T(8,128)(2,1)} %get-tuple-element.60.refs_3_.refs_4_), custom_call_target="tpu_custom_call" | custom-call | flops 2013265920 | bytes 7077888 | tf_op jit(solution)/shard_map/pallas_call | solution.py:324
  61.0 7.2 %all-to-all-start.1 = ((bf16[32,8,2560]{2,1,0:T(8,128)(2,1)}), bf16[32,8,2560]{2,1,0:T(8,128)(2,1)}, u32[]{:S(2)}, u32[]{:S(2)}) async-start(bf16[32,8,2560]{2,1,0:T(8,128)(2,1)} %bitcast.41), calls=%async_computation.1 | async-start | bytes 2621440 | tf_op jit(solution)/shard_map/all_to_all | solution.py:625
  68.2 5.4 %shard_map.121 = (f32[640,512]{1,0:T(8,128)}, f32[640,512]{1,0:T(8,128)}, bf16[640,512]{1,0:T(8,128)(2,1)}, bf16[640,1024]{1,0:T(8,128)(2,1)}, bf16[640,1024]{1,0:T(8,128)(2,1)}) custom-call(bf16[256,5120]{1,0:T(8,128)(2,1)} %bitcast.10.refs_0_, bf16[1024,512]{1,0:T(8,128)(2,1)} %get-tuple-element.58.refs_1_.refs_7_, ...), custom_call_target="tpu_custom_call" | custom-call | flops 1342177280 | bytes 10616832 | tf_op jit(solution)/shard_map/pallas_call | solution.py:324
  73.6 14.9 %all-to-all-done.1 = bf16[32,8,2560]{2,1,0:T(8,128)(2,1)} async-done(((bf16[32,8,2560]{2,1,0:T(8,128)(2,1)}), bf16[32,8,2560]{2,1,0:T(8,128)(2,1)}, u32[]{:S(2)}, u32[]{:S(2)}) %all-to-all-start.1) | async-done | bytes 1310752 | tf_op jit(solution)/shard_map/all_to_all | solution.py:625
  88.6 5.1 %shard_map.122 = (bf16[64,1024]{1,0:T(8,128)(2,1)}, bf16[256,2688]{1,0:T(8,128)(2,1)}, f32[64,32]{1,0:T(8,128)}) custom-call(bf16[64,1024]{1,0:T(8,128)(2,1)} %get-tuple-element.55.refs_0_.refs_5_, s32[64,8]{1,0:T(8,128)} %get-tuple-element.112.refs_3_.refs_1_.refs_6_, f32[64,32]{1,0:T(8,128)} %get-tuple-element.56.refs_2_.refs_7_, ...), custom_call_target="tpu_custom_call" | custom-call | flops 600000000 | bytes 3108864 | tf_op jit(solution)/shard_map/pallas_call | solution.py:324
  93.6 24.6 %all_to_all.62 = bf16[32,8,2688]{2,1,0:T(8,128)(2,1)} all-to-all(bf16[32,8,2688]{2,1,0:T(8,128)(2,1)} %bitcast.40), channel_id=1, replica_groups=mesh['dp'=2,'pipe'=2,'expert'=32] {'expert'}, dimensions={0} | all-to-all | bytes 2752512 | tf_op jit(solution)/shard_map/all_to_all | solution.py:625
  118.2 9.3 %shard_map.123 = (bf16[256,2688]{1,0:T(8,128)(2,1)}, bf16[640,1024]{1,0:T(8,128)(2,1)}, bf16[640,1024]{1,0:T(8,128)(2,1)}, bf16[640,512]{1,0:T(8,128)(2,1)}, bf1...) custom-call(bf16[256,2688]{1,0:T(8,128)(2,1)} %bitcast.39, bf16[640,1024]{1,0:T(8,128)(2,1)} %get-tuple-element.68.refs_1_, ...), custom_call_target="tpu_custom_call" | custom-call | flops 4026531840 | bytes 11796480 | tf_op jit(solution)/shard_map/pallas_call | solution.py:324
  127.6 4.7 %all-to-all-start.3 = ((bf16[32,8,2688]{2,1,0:T(8,128)(2,1)}), bf16[32,8,2688]{2,1,0:T(8,128)(2,1)}, u32[]{:S(2)}, u32[]{:S(2)}) async-start(bf16[32,8,2688]{2,1,0:T(8,128)(2,1)} %bitcast.38), calls=%async_computation.3 | async-start | bytes 2752512 | tf_op jit(solution)/shard_map/all_to_all | solution.py:625
  132.3 6.6 %shard_map.125 = (bf16[768,512]{1,0:T(8,128)(2,1)}, bf16[768,512]{1,0:T(8,128)(2,1)}, bf16[768,512]{1,0:T(8,128)(2,1)}, bf16[768,512]{1,0:T(8,128)(2,1)}) custom-call(s32[2]{0:T(128)} %pad_add_fusion.refs_0_, bf16[640,512]{1,0:T(8,128)(2,1)} %get-tuple-element.75.refs_1_, bf16[640,512]{1,0:T(8,128)(2,1)} %get-tuple-element.76.refs_2_, ...), custom_call_target="tpu_custom_call" | custom-call | flops 2013265920 | bytes 7733248 | tf_op jit(solution)/shard_map/pallas_call | solution.py:324
  139.5 12.1 %all-to-all-done.3 = bf16[32,8,2688]{2,1,0:T(8,128)(2,1)} async-done(((bf16[32,8,2688]{2,1,0:T(8,128)(2,1)}), bf16[32,8,2688]{2,1,0:T(8,128)(2,1)}, u32[]{:S(2)}, u32[]{:S(2)}) %all-to-all-start.3) | async-done | bytes 1376288 | tf_op jit(solution)/shard_map/all_to_all | solution.py:625
  151.5 6.8 %shard_map.124 = (bf16[256,2688]{1,0:T(8,128)(2,1)}, f32[2,1024]{1,0:T(2,128)}) custom-call(bf16[64,1024]{1,0:T(8,128)(2,1)} %get-tuple-element.65.refs_0_, s32[64,8]{1,0:T(8,128)} %get-tuple-element.111.refs_4_.refs_1_, f32[64,32]{1,0:T(8,128)} %get-tuple-element.66.refs_2_, bf16[256,2688]{1,0:T(8,128)(2,1)} %bitcast.19.refs_3_, ...), custom_call_target="tpu_custom_call" | custom-call | flops 900000000 | bytes 4624384 | tf_op jit(solution)/shard_map/pallas_call | solution.py:324
  158.3 5.1 %all-to-all-start.4 = ((bf16[32,8,2688]{2,1,0:T(8,128)(2,1)}), bf16[32,8,2688]{2,1,0:T(8,128)(2,1)}, u32[]{:S(2)}, u32[]{:S(2)}) async-start(bf16[32,8,2688]{2,1,0:T(8,128)(2,1)} %bitcast.37), calls=%async_computation.4 | async-start | bytes 2752512 | tf_op jit(solution)/shard_map/all_to_all | solution.py:625
  167.1 1.3 add_convert_fusion.2
  169.1 4.1 %collective-permute-start.9 = (bf16[768,512]{1,0:T(8,128)(2,1)S(1)}, bf16[768,512]{1,0:T(8,128)(2,1)}, u32[]{:S(2)}, u32[]{:S(2)}) collective-permute-start(bf16[768,512]{1,0:T(8,128)(2,1)S(1)} %add_convert_fusion.2), channel_id=1, source_target_pairs={{0,96},{64,32},{1,97},{65,33},{2,98},{66,34},{3,99},{67,35},{4,100... | collective-permute-start | bytes 2359304 | tf_op jit(solution)/shard_map/ppermute | solution.py:713
  175.0 17.6 %collective-permute-done.9.refs_7_ = bf16[768,512]{1,0:T(8,128)(2,1)} collective-permute-done((bf16[768,512]{1,0:T(8,128)(2,1)S(1)}, bf16[768,512]{1,0:T(8,128)(2,1)}, u32[]{:S(2)}, u32[]{:S(2)}) %collective-permute-start.9) | collective-permute-done | bytes 786464 | tf_op jit(solution)/shard_map/ppermute | solution.py:713
  192.6 9.5 %shard_map.126 = (bf16[768,512]{1,0:T(8,128)(2,1)}, bf16[768,512]{1,0:T(8,128)(2,1)}, bf16[768,512]{1,0:T(8,128)(2,1)}, bf16[768,512]{1,0:T(8,128)(2,1)}, f32[2,1024]{1,0:T(2,128)}, /*index=5*/f32[2,1024]{1,0:T(2,128)}) custom-call(s32[2]{0:T(128)} %pad_add_fusion.refs_0_, bf16[256,2688]{1,0:T(8,128)(2,1)} %bitcast.21.refs_1_, ...), custom_call_target="tpu_custom_call" | custom-call | flops 3019898880 | bytes 13598720 | tf_op jit(solution)/shard_map/pallas_call | solution.py:324
  202.1 3.2 %collective-permute-start.11 = (bf16[768,512]{1,0:T(8,128)(2,1)}, bf16[768,512]{1,0:T(8,128)(2,1)S(1)}, u32[]{:S(2)}, u32[]{:S(2)}) collective-permute-start(bf16[768,512]{1,0:T(8,128)(2,1)} %get-tuple-element.91), channel_id=1, source_target_pairs={{0,32},{32,0},{1,33},{33,1},{2,34},{34,2},{3,35},{35,3},{4,36},{36... | collective-permute-start | bytes 2359304 | tf_op jit(solution)/shard_map/ppermute | solution.py:629
  205.4 2.0 collective-permute-done.11
  208.8 1.4 collective-permute-start.12
  212.6 2.7 %collective-permute-start.14 = (bf16[768,512]{1,0:T(8,128)(2,1)}, bf16[768,512]{1,0:T(8,128)(2,1)}, u32[]{:S(2)}, u32[]{:S(2)}) collective-permute-start(bf16[768,512]{1,0:T(8,128)(2,1)} %add_convert_fusion), channel_id=1, source_target_pairs={{0,64},{64,0},{1,65},{65,1},{2,66},{66,2},{3,67},{67,3},{4,68},{68... | collective-permute-start | bytes 2359304 | tf_op jit(solution)/shard_map/ppermute | solution.py:713
  215.3 1.7 collective-permute-start.16
  218.5 1.9 shard_map.128
  220.4 24.3 %all_to_all.63.refs_0_ = f32[64,16,128]{2,1,0:T(8,128)} all-to-all(f32[64,16,128]{2,1,0:T(8,128)} %shard_map.128), channel_id=1, replica_groups=mesh['dp'=2,'pipe'=2,'expert'=32] {'dp','expert'}, dimensions={0} | all-to-all | bytes 1048576 | tf_op jit(solution)/shard_map/all_to_all | solution.py:750
  244.7 2.0 shard_map.129
  246.7 3.5 %shard_map.127 = (bf16[512,512]{1,0:T(8,128)(2,1)}, bf16[512,512]{1,0:T(8,128)(2,1)}, bf16[512,512]{1,0:T(8,128)(2,1)}) custom-call(s32[2]{0:T(128)} %pad_add_fusion.refs_0_, bf16[768,512]{1,0:T(8,128)(2,1)} %copy-done.1, bf16[768,512]{1,0:T(8,128)(2,1)} %collective-permute-done.12.refs_2_, bf16[768,512]{1,0:T(8,128)(2,1)} %collective-permute-done.14.refs_3_, ...), custom_call_target="tpu_custom_call" | custom-call | flops 1000 | bytes 4718592 | tf_op jit(solution)/shard_map/pallas_call | solution.py:324
  (65 shorter events, 16.2 us)
Async XLA Ops:
  0.6 2.9 %collective-permute-start.1 = (f32[1,1024]{1,0:T(1,128)}, f32[1,1024]{1,0:T(1,128)S(1)}, u32[]{:S(2)}, u32[]{:S(2)}) collective-permute-start(f32[1,1024]{1,0:T(1,128)} %refs_5_.1), channel_id=1, source_target_pairs={{0,32},{32,0},{1,33},{33,1},{2,34},{34,2},{3,35},{35,3},{4,36},{36... | collective-permute-start | bytes 12296 | tf_op jit(solution)/shard_map/ppermute | solution.py:629
  1.5 1.4 collective-permute-start
  2.1 1.5 collective-permute-start.2
  8.6 9.8 %copy-start.2 = (bf16[1,1,512,1024]{3,2,1,0:T(8,128)(2,1)S(1)}, bf16[1,1,512,1024]{3,2,1,0:T(8,128)(2,1)}, u32[]{:S(2)}) copy-start(bf16[1,1,512,1024]{3,2,1,0:T(8,128)(2,1)} %param.14) | copy-start | bytes 3145732
  8.6 10.0 %copy-start.3 = (bf16[1,1,1024,512]{3,2,1,0:T(8,128)(2,1)S(1)}, bf16[1,1,1024,512]{3,2,1,0:T(8,128)(2,1)}, u32[]{:S(2)}) copy-start(bf16[1,1,1024,512]{3,2,1,0:T(8,128)(2,1)} %param.13) | copy-start | bytes 3145732
  8.6 10.4 %copy-start.4 = (bf16[1,1,1024,512]{3,2,1,0:T(8,128)(2,1)S(1)}, bf16[1,1,1024,512]{3,2,1,0:T(8,128)(2,1)}, u32[]{:S(2)}) copy-start(bf16[1,1,1024,512]{3,2,1,0:T(8,128)(2,1)} %param.12) | copy-start | bytes 3145732
  8.6 46.7 %all-to-all-start = ((bf16[32,8,5120]{2,1,0:T(8,128)(2,1)}), bf16[32,8,5120]{2,1,0:T(8,128)(2,1)}, u32[]{:S(2)}, u32[]{:S(2)}) async-start(bf16[32,8,5120]{2,1,0:T(8,128)(2,1)} %bitcast.36), calls=%async_computation | async-start | bytes 5242880 | tf_op jit(solution)/shard_map/all_to_all | solution.py:625
  18.4 2.7 %collective-permute-start.5 = (bf16[512,1024]{1,0:T(8,128)(2,1)S(1)}, bf16[512,1024]{1,0:T(8,128)(2,1)S(1)}, u32[]{:S(2)}, u32[]{:S(2)}) collective-permute-start(bf16[512,1024]{1,0:T(8,128)(2,1)S(1)} %bitcast.42), channel_id=1, source_target_pairs={{0,32},{32,0},{1,33},{33,1},{2,34},{34,2},{3,35},{35,3},{4,36},{36... | collective-permute-start | bytes 3145736 | tf_op jit(solution)/shard_map/ppermute | solution.py:629
  18.6 4.1 %collective-permute-start.4 = (bf16[1024,512]{1,0:T(8,128)(2,1)S(1)}, bf16[1024,512]{1,0:T(8,128)(2,1)S(1)}, u32[]{:S(2)}, u32[]{:S(2)}) collective-permute-start(bf16[1024,512]{1,0:T(8,128)(2,1)S(1)} %bitcast.43), channel_id=1, source_target_pairs={{0,32},{32,0},{1,33},{33,1},{2,34},{34,2},{3,35},{35,3},{4,36},{36... | collective-permute-start | bytes 3145736 | tf_op jit(solution)/shard_map/ppermute | solution.py:629
  19.0 5.2 %collective-permute-start.3 = (bf16[1024,512]{1,0:T(8,128)(2,1)S(1)}, bf16[1024,512]{1,0:T(8,128)(2,1)S(1)}, u32[]{:S(2)}, u32[]{:S(2)}) collective-permute-start(bf16[1024,512]{1,0:T(8,128)(2,1)S(1)} %bitcast.44), channel_id=1, source_target_pairs={{0,32},{32,0},{1,33},{33,1},{2,34},{34,2},{3,35},{35,3},{4,36},{36... | collective-permute-start | bytes 3145736 | tf_op jit(solution)/shard_map/ppermute | solution.py:629
  61.0 27.5 %all-to-all-start.1 = ((bf16[32,8,2560]{2,1,0:T(8,128)(2,1)}), bf16[32,8,2560]{2,1,0:T(8,128)(2,1)}, u32[]{:S(2)}, u32[]{:S(2)}) async-start(bf16[32,8,2560]{2,1,0:T(8,128)(2,1)} %bitcast.41), calls=%async_computation.1 | async-start | bytes 2621440 | tf_op jit(solution)/shard_map/all_to_all | solution.py:625
  127.6 23.9 %all-to-all-start.3 = ((bf16[32,8,2688]{2,1,0:T(8,128)(2,1)}), bf16[32,8,2688]{2,1,0:T(8,128)(2,1)}, u32[]{:S(2)}, u32[]{:S(2)}) async-start(bf16[32,8,2688]{2,1,0:T(8,128)(2,1)} %bitcast.38), calls=%async_computation.3 | async-start | bytes 2752512 | tf_op jit(solution)/shard_map/all_to_all | solution.py:625
  138.9 24.6 %collective-permute-start.6 = (bf16[768,512]{1,0:T(8,128)(2,1)}, bf16[768,512]{1,0:T(8,128)(2,1)S(1)}, u32[]{:S(2)}, u32[]{:S(2)}) collective-permute-start(bf16[768,512]{1,0:T(8,128)(2,1)} %get-tuple-element.81), channel_id=1, source_target_pairs={{0,32},{32,0},{1,33},{33,1},{2,34},{34,2},{3,35},{35,3},{4,36},{36... | collective-permute-start | bytes 2359304 | tf_op jit(solution)/shard_map/ppermute | solution.py:629
  139.0 28.1 %collective-permute-start.8 = (bf16[768,512]{1,0:T(8,128)(2,1)}, bf16[768,512]{1,0:T(8,128)(2,1)}, u32[]{:S(2)}, u32[]{:S(2)}) collective-permute-start(bf16[768,512]{1,0:T(8,128)(2,1)} %get-tuple-element.83), channel_id=1, source_target_pairs={{0,32},{32,0},{1,33},{33,1},{2,34},{34,2},{3,35},{35,3},{4,36},{36... | collective-permute-start | bytes 2359304 | tf_op jit(solution)/shard_map/ppermute | solution.py:629
  158.3 6.0 %copy-start.8 = (bf16[768,512]{1,0:T(8,128)(2,1)S(1)}, bf16[768,512]{1,0:T(8,128)(2,1)}, u32[]{:S(2)}) copy-start(bf16[768,512]{1,0:T(8,128)(2,1)} %get-tuple-element.80) | copy-start | bytes 2359300
  158.3 34.2 %all-to-all-start.4 = ((bf16[32,8,2688]{2,1,0:T(8,128)(2,1)}), bf16[32,8,2688]{2,1,0:T(8,128)(2,1)}, u32[]{:S(2)}, u32[]{:S(2)}) async-start(bf16[32,8,2688]{2,1,0:T(8,128)(2,1)} %bitcast.37), calls=%async_computation.4 | async-start | bytes 2752512 | tf_op jit(solution)/shard_map/all_to_all | solution.py:625
  163.4 3.6 %copy-start.7 = (bf16[768,512]{1,0:T(8,128)(2,1)S(1)}, bf16[768,512]{1,0:T(8,128)(2,1)}, u32[]{:S(2)}) copy-start(bf16[768,512]{1,0:T(8,128)(2,1)} %get-tuple-element.82) | copy-start | bytes 2359300
  163.4 0.9 copy-start.10
  165.7 36.4 %copy-start = (bf16[768,512]{1,0:T(8,128)(2,1)}, bf16[768,512]{1,0:T(8,128)(2,1)S(1)}, u32[]{:S(2)}) copy-start(bf16[768,512]{1,0:T(8,128)(2,1)S(1)} %add_convert_fusion.3.refs_6_) | copy-start | bytes 2359300
  165.7 7.6 %collective-permute-start.7 = (bf16[768,512]{1,0:T(8,128)(2,1)S(1)}, bf16[768,512]{1,0:T(8,128)(2,1)S(1)}, u32[]{:S(2)}, u32[]{:S(2)}) collective-permute-start(bf16[768,512]{1,0:T(8,128)(2,1)S(1)} %add_convert_fusion.3.refs_6_), channel_id=1, source_target_pairs={{0,32},{1,33},{2,34},{3,35},{4,36},{5,37},{6,38},{7,39},{8,40},{9,... | collective-permute-start | bytes 2359304 | tf_op jit(solution)/shard_map/ppermute | solution.py:732
  168.4 5.8 %collective-permute-start.10 = (bf16[768,512]{1,0:T(8,128)(2,1)S(1)}, bf16[768,512]{1,0:T(8,128)(2,1)S(1)}, u32[]{:S(2)}, u32[]{:S(2)}) collective-permute-start(bf16[768,512]{1,0:T(8,128)(2,1)S(1)} %add_convert_fusion.2), channel_id=1, source_target_pairs={{32,96},{96,32},{33,97},{97,33},{34,98},{98,34},{35,99},{99,35},{3... | collective-permute-start | bytes 2359304 | tf_op jit(solution)/shard_map/ppermute | solution.py:713
  169.1 23.5 %collective-permute-start.9 = (bf16[768,512]{1,0:T(8,128)(2,1)S(1)}, bf16[768,512]{1,0:T(8,128)(2,1)}, u32[]{:S(2)}, u32[]{:S(2)}) collective-permute-start(bf16[768,512]{1,0:T(8,128)(2,1)S(1)} %add_convert_fusion.2), channel_id=1, source_target_pairs={{0,96},{64,32},{1,97},{65,33},{2,98},{66,34},{3,99},{67,35},{4,100... | collective-permute-start | bytes 2359304 | tf_op jit(solution)/shard_map/ppermute | solution.py:713
  173.3 0.9 copy-start.5
  202.1 8.2 %copy-start.9 = (bf16[768,512]{1,0:T(8,128)(2,1)S(1)}, bf16[768,512]{1,0:T(8,128)(2,1)}, u32[]{:S(2)}) copy-start(bf16[768,512]{1,0:T(8,128)(2,1)} %get-tuple-element.92) | copy-start | bytes 2359300
  202.1 5.3 %collective-permute-start.11 = (bf16[768,512]{1,0:T(8,128)(2,1)}, bf16[768,512]{1,0:T(8,128)(2,1)S(1)}, u32[]{:S(2)}, u32[]{:S(2)}) collective-permute-start(bf16[768,512]{1,0:T(8,128)(2,1)} %get-tuple-element.91), channel_id=1, source_target_pairs={{0,32},{32,0},{1,33},{33,1},{2,34},{34,2},{3,35},{35,3},{4,36},{36... | collective-permute-start | bytes 2359304 | tf_op jit(solution)/shard_map/ppermute | solution.py:629
  205.3 4.9 %collective-permute-start.13 = (bf16[768,512]{1,0:T(8,128)(2,1)}, bf16[768,512]{1,0:T(8,128)(2,1)S(1)}, u32[]{:S(2)}, u32[]{:S(2)}) collective-permute-start(bf16[768,512]{1,0:T(8,128)(2,1)} %get-tuple-element.93), channel_id=1, source_target_pairs={{0,32},{32,0},{1,33},{33,1},{2,34},{34,2},{3,35},{35,3},{4,36},{36... | collective-permute-start | bytes 2359304 | tf_op jit(solution)/shard_map/ppermute | solution.py:629
  208.8 35.9 %copy-start.1 = (bf16[768,512]{1,0:T(8,128)(2,1)}, bf16[768,512]{1,0:T(8,128)(2,1)S(1)}, u32[]{:S(2)}) copy-start(bf16[768,512]{1,0:T(8,128)(2,1)S(1)} %add_convert_fusion.1.refs_1_) | copy-start | bytes 2359300
  208.8 6.5 %copy-start.13 = (f32[2,1024]{1,0:T(2,128)S(1)}, f32[2,1024]{1,0:T(2,128)}, u32[]{:S(2)}) copy-start(f32[2,1024]{1,0:T(2,128)} %get-tuple-element.102) | copy-start | bytes 24580
  208.8 37.9 %collective-permute-start.12 = (bf16[768,512]{1,0:T(8,128)(2,1)S(1)}, bf16[768,512]{1,0:T(8,128)(2,1)}, u32[]{:S(2)}, u32[]{:S(2)}) collective-permute-start(bf16[768,512]{1,0:T(8,128)(2,1)S(1)} %add_convert_fusion.1.refs_1_), channel_id=1, source_target_pairs={{32,0},{33,1},{34,2},{35,3},{36,4},{37,5},{38,6},{39,7},{40,8},{41... | collective-permute-start | bytes 2359304 | tf_op jit(solution)/shard_map/ppermute | solution.py:752
  211.3 35.3 %collective-permute-start.15 = (bf16[768,512]{1,0:T(8,128)(2,1)}, bf16[768,512]{1,0:T(8,128)(2,1)}, u32[]{:S(2)}, u32[]{:S(2)}) collective-permute-start(bf16[768,512]{1,0:T(8,128)(2,1)} %add_convert_fusion), channel_id=1, source_target_pairs={{32,64},{96,0},{33,65},{97,1},{34,66},{98,2},{35,67},{99,3},{36,68... | collective-permute-start | bytes 2359304 | tf_op jit(solution)/shard_map/ppermute | solution.py:713
  212.6 34.0 %collective-permute-start.14 = (bf16[768,512]{1,0:T(8,128)(2,1)}, bf16[768,512]{1,0:T(8,128)(2,1)}, u32[]{:S(2)}, u32[]{:S(2)}) collective-permute-start(bf16[768,512]{1,0:T(8,128)(2,1)} %add_convert_fusion), channel_id=1, source_target_pairs={{0,64},{64,0},{1,65},{65,1},{2,66},{66,2},{3,67},{67,3},{4,68},{68... | collective-permute-start | bytes 2359304 | tf_op jit(solution)/shard_map/ppermute | solution.py:713
  215.3 2.6 %collective-permute-start.16 = (f32[2,1024]{1,0:T(2,128)S(1)}, f32[2,1024]{1,0:T(2,128)S(1)}, u32[]{:S(2)}, u32[]{:S(2)}) collective-permute-start(f32[2,1024]{1,0:T(2,128)S(1)} %copy-done.13), channel_id=1, source_target_pairs={{0,32},{32,0},{1,33},{33,1},{2,34},{34,2},{3,35},{35,3},{4,36},{36... | collective-permute-start | bytes 24584 | tf_op jit(solution)/shard_map/ppermute | solution.py:629
  (4 other events, 2.7 us)
where the time goes:
time: 252 us; the launch traced here: 250 us
  waiting for transfers between devices  79.3 us (31%)
  Pallas kernels  60 us (24%)
  blocking collectives  48.9 us (19%)
  starting transfers between devices  45.3 us (18%)
  other arithmetic  10.9 us (4%)
  local copies, waits for them, and re-layouts  4.79 us (2%)
    pallas_call x11, Pallas kernels, call(): pl.pallas_call(kernel, out_shape=out_shape, in_specs=[pl.BlockSpec(memory...  60 us
    all_to_all x4, waiting for transfers between devices, exchanged(): lax.all_to_all(rows, 'expert', split_axis=0, concat_axis=0, tiled=True)  56.7 us
    all_to_all x4, starting transfers between devices, exchanged(): lax.all_to_all(rows, 'expert', split_axis=0, concat_axis=0, tiled=True)  26.7 us
    all_to_all x1, blocking collectives, exchanged(): lax.all_to_all(rows, 'expert', split_axis=0, concat_axis=0, tiled=True)  24.6 us
    all_to_all x1, blocking collectives, shards(): lax.all_to_all(told, ('dp', 'expert'), split_axis=0, concat_axis=0, tiled...  24.3 us
    ppermute x4, waiting for transfers between devices, to_owner(): lax.ppermute(paired, ('dp', 'pipe'), [(2 * d + p, 2 * (1 - d) + owner) fo...  17.6 us
    ppermute x4, starting transfers between devices, to_owner(): lax.ppermute(paired, ('dp', 'pipe'), [(2 * d + p, 2 * (1 - d) + owner) fo...  8.82 us
    ppermute x11, starting transfers between devices, swapped(): return lax.ppermute(value, 'pipe', [(0, 1), (1, 0)])  7.03 us
  transfers between devices with their start and end apart: 21, of which 7 were waited for; matrix products, arithmetic and copies ran while one was open for 5% of the time, Pallas kernels for 9%

commit v1 on v0

--- a/solution.py
+++ b/solution.py
@@ -92,18 +92,27 @@
     return flags(column_place(shape, 0)[0] == count(shape, 1))
 
 
-def slots_of(picks, expand):
-    columns = lax.broadcasted_iota(jnp.int32, (TOK, EXP), 1)
-    mask = jnp.zeros((TOK, EXP), F32)
-    for k in range(picks.shape[1]):
-        mask = mask + jnp.where(picks[:, k : k + 1] == columns, 1.0, 0.0)
+def mask_of(picks):
+    shape = (EXP, ROWS)
+    experts = lax.broadcasted_iota(jnp.int32, shape, 0)
+    same = flags(experts == lax.broadcasted_iota(jnp.int32, shape, 1))
+    masks = []
+    for v in picks:
+        mask = jnp.zeros(shape, F32)
+        for k in range(v.shape[0]):
+            mask = mask + jnp.where(v[k : k + 1, :] == experts, 1.0, 0.0)
+        masks.append(dot_t0(mask.astype(BF), same))
+    return jnp.concatenate(masks, axis=0)
+
+
+def slots_of(mask, expand):
     row = lax.broadcasted_iota(jnp.int32, (TOK, TOK), 0)
     column = lax.broadcasted_iota(jnp.int32, (TOK, TOK), 1)
     earlier = flags((column < row) & ((row < ROWS) | (column >= ROWS)))
     start = jnp.where(lax.broadcasted_iota(jnp.int32, (TOK, EXP), 0) < ROWS, 0.0, 1.0 * CAP)
     slot = mask * (dot(earlier, mask.astype(BF)) + start + 1.0) - 1.0
     table = dot(slot.astype(BF), expand) == column_place((1, 4 * PACK), 1)[1]
-    return mask, table, slot
+    return table, slot
 
 
 def norm(tokens, gain):
@@ -281,17 +290,15 @@
                 copy.wait()
 
 
-def call(body, outs, args, flops, at=None, scratch=(), order=None):
+def call(body, outs, args, flops, scratch=(), order=None):
     args = [v if isinstance(v, Load) else Load(v) for v in args]
     others = [v.other for v in args if v.other is not None]
     out_shape = [jax.ShapeDtypeStruct(out[0], out[1]) for out in outs]
     ways = [(out[2], cuts(out[3])) if len(out) > 2 else (0, [(0, out[0][0])]) for out in outs]
-    scalars = [] if at is None else [at]
     n, m = len(args), len(outs)
 
     def kernel(*refs):
-        where = refs[0] if scalars else None
-        refs = refs[len(scalars) :]
+        where = (lax.axis_index("pipe"), lax.axis_index("dp"))
         ins, twins, refs = refs[:n], refs[n : n + len(others)], refs[n + len(others) :]
         results, held, refs = refs[:m], refs[m : m + n], refs[m + n :]
         made, load_sems, store_sems = refs[:m], refs[m : m + n], refs[m + n : m + n + m]
@@ -306,14 +313,17 @@
         ]
         moves = Moves(loads, stores)
         if others:
-            for pick, sources in enumerate((ins, twins)):
+            second = iter(twins)
+            second = [src if v.other is None else next(second) for v, src in zip(args, ins)]
+            for pick, sources in enumerate((ins, second)):
 
                 @pl.when(where[0] == pick)
                 def _():
                     picked = [v.copies(*way, where) for v, *way in zip(args, sources, held, load_sems)]
-                    for piece in range(len(args[0].cuts)):
+                    for piece in range(max(len(copies) for copies in picked)):
                         for copies in picked:
-                            copies[piece].start()
+                            if piece < len(copies):
+                                copies[piece].start()
 
         else:
             moves.start(order)
@@ -324,7 +334,7 @@
     return pl.pallas_call(
         kernel,
         out_shape=out_shape,
-        in_specs=[pl.BlockSpec(memory_space=pltpu.SMEM)] * len(scalars) + [hbm] * (n + len(others)),
+        in_specs=[hbm] * (n + len(others)),
         out_specs=[hbm] * m,
         scratch_shapes=[pltpu.VMEM(v.shape, v.dtype) for v in args]
         + [pltpu.VMEM(s.shape, s.dtype) for s in out_shape]
@@ -333,17 +343,23 @@
         + list(scratch),
         cost_estimate=cost(flops, [v.array for v in args] + out_shape),
         compiler_params=pltpu.CompilerParams(vmem_limit_bytes=63 << 20),
-    )(*scalars, *[v.array for v in args], *others)
+    )(*[v.array for v in args], *others)
 
 
 def start_body(moves, at, ins, outs):
-    inputs, cotangent, picks0, picks1, gain_own, gain_other, router_own, router_other = ins
-    send, weights, tokens, grad, gains, routers = outs
+    inputs, cotangent, picks_own, picks_other, gain_own, gain_other, router_own, router_other = ins
+    send, weights, tokens, grad, gains, routers, mask0_out, mask1_out = outs
     mine = at[0] == 0
     expand = expand_of()
     moves.need(2, 3)
-    mask, table0, _ = slots_of(picks0[...], expand)
-    table1 = slots_of(picks1[...], expand)[1]
+    own = [picks_own[HALF * at[0] + i] for i in range(HALF)]
+    other = [picks_other[HALF * at[0] + i] for i in range(HALF)]
+    mask = mask_of([jnp.where(mine, v, w) for v, w in zip(own, other)])
+    mask1 = mask_of([jnp.where(mine, w, v) for v, w in zip(own, other)])
+    mask0_out[...] = mask
+    mask1_out[...] = mask1
+    table0 = slots_of(mask, expand)[0]
+    table1 = slots_of(mask1, expand)[0]
     moves.need(0, 1, 4, 5)
     own, other = gain_own[...], gain_other[...]
     gain0 = jnp.where(mine, own, other)
@@ -361,7 +377,7 @@
     routers[0:EXP, :] = router0
     routers[EXP:, :] = jnp.where(mine, other, own)
     weights[...] = mix(normed, router0, mask)
-    moves.flush(0, 1, 2, 3, 4, 5)
+    moves.flush(0, 1, 2, 3, 4, 5, 6, 7)
 
 
 def forward_body(moves, at, ins, outs, rows):
@@ -524,22 +540,18 @@
     moves.flush(0, 0)
 
 
-def heard_body(moves, at, ins, outs):
-    (heard,) = ins
-    router, gain = outs
-    moves.need(0)
+def finish_body(moves, at, ins, outs):
+    low, high, low_got, high_got, heard = ins
+    router, gain = outs[3:]
+    moves.need(4)
     _, lines, lane = heard.shape
     for j in range(lines // 2):
         column = slice(j * lane, (j + 1) * lane)
         router[:, column] = heard[0:EXP, j, :] + heard[EXP:, j, :]
         gain[:, column] = jnp.sum(heard[:, lines // 2 + j, :], axis=0, keepdims=True)
-    moves.flush(0, 0, 1)
-
-
-def finish_body(moves, at, ins, outs):
-    low, high, low_got, high_got = ins
+    moves.flush(0, 3, 4)
     quarter = low.shape[0] // 3
-    for i, out in enumerate(outs):
+    for i, out in enumerate(outs[:3]):
         moves.need(*[(k, i) for k in range(4)])
         rows = slice(i * quarter, (i + 1) * quarter)
         out[0:quarter, :] = (low[rows, :].astype(F32) + low_got[rows, :].astype(F32)).astype(BF)
@@ -548,19 +560,19 @@
 
 
 def middle_body(moves, at, ins, outs):
-    tokens, picks0, weights0, returned, picks1, gains, routers = ins
+    tokens, mask0, weights0, returned, mask1, gains, routers = ins
     mixed_out, send, weights1 = outs
     width = tokens.shape[1]
     expand = expand_of()
     moves.need(1, 2, 4)
-    _, table0, _ = slots_of(picks0[...], expand)
+    table0 = slots_of(mask0[...], expand)[0]
     parts = weighted(table0, split2(weights0[...]), expand)
-    mask1, table1, _ = slots_of(picks1[...], expand)
+    table1 = slots_of(mask1[...], expand)[0]
     moves.need(0, 3, 5, 6)
     mixed = (tokens[...].astype(F32) + from_packed(parts, returned, width)).astype(BF)
     mixed_out[...] = mixed
     normed, _, _ = norm(mixed, gains[1:2, :])
-    weights = mix(normed, routers[EXP:, :], mask1)
+    weights = mix(normed, routers[EXP:, :], mask1[...])
     weights1[...] = weights
     send[:, send.shape[1] - LANE :] = small_lines(weighted(table1, split2(weights), expand))
     to_packed([flags(table1)], normed, send, lambda i: moves.flush(i, 1))
@@ -568,15 +580,15 @@
 
 
 def turn_body(moves, at, ins, outs):
-    tokens1, picks1, weights1, returned1, grad, tokens0, picks0, weights0, returned0, gains, routers = ins
+    tokens1, mask1, weights1, returned1, grad, tokens0, mask0, weights0, returned0, gains, routers = ins
     send, gains_out = outs
     width = tokens1.shape[1]
     half = width // 2
     expand = expand_of()
     moves.need(0, 1, 2, 4, 5, 6, 7, 9, 10)
     gain0, gain1 = gains[0:1, :], gains[1:2, :]
-    _, table1, slot1 = slots_of(picks1[...], expand)
-    _, table0, _ = slots_of(picks0[...], expand)
+    table1, slot1 = slots_of(mask1[...], expand)
+    table0 = slots_of(mask0[...], expand)[0]
     w0, w1 = weights0[...], weights1[...]
     parts0 = weighted(table0, split2(w0), expand)
     _, scale0, values0 = norm(tokens0[...], gain0)
@@ -631,21 +643,16 @@
 
 def shards(inputs, cotangent, norm_gain, w_router, w_gate, w_up, w_down, routes):
     pipe = lax.axis_index("pipe")
-    data = lax.axis_index("dp")
-    at = jnp.stack([pipe, data]).astype(jnp.int32)
     width = inputs.shape[-1]
     inner = w_gate.shape[-1]
     half, quarter = width // 2, width // 4
     first = pipe == 0
     flops = ALL * width * inner
 
-    def part_of(v, which):
-        return lax.dynamic_slice_in_dim(v, which * HALF, HALF, 0).reshape(TOK, -1)
-
     def both(own, other):
         return jnp.where(first, own, other), jnp.where(first, other, own)
 
-    picks0, picks1 = both(part_of(routes[0], pipe), swapped(part_of(routes[0], 1 - pipe)))
+    picks = routes[0].transpose(0, 2, 1)
     router = w_router[0].T
     packed = 2 * width + half
     pieces = (width, width, half)
@@ -656,21 +663,20 @@
     wide_shape = ((ALL, inner), F32, 0, part_rows)
     small_shape = ((PACK, packed + LANE), BF, 1, with_small)
     few = ((TOK, width), BF)
-    send0, weights0, tokens0, grad1, gains, routers = call(
+    send0, weights0, tokens0, grad1, gains, routers, mask0, mask1 = call(
         start_body,
-        [((PACK, 2 * packed), BF, 1, pieces * 2), ((TOK, EXP), F32), few, few, ((2, width), F32), ((2 * EXP, width), BF)],
+        [((PACK, 2 * packed), BF, 1, pieces * 2), ((TOK, EXP), F32), few, few, ((2, width), F32), ((2 * EXP, width), BF)] + [((TOK, EXP), F32)] * 2,
         [
             Tokens(inputs.reshape(-1, width)),
             Tokens(cotangent.reshape(-1, width)),
-            picks0,
-            picks1,
+            picks,
+            swapped(picks),
             norm_gain,
             swapped(norm_gain),
             router,
             swapped(router),
         ],
         400_000_000,
-        at,
     )
     arrived = exchanged(send0)
     mats = [both(w[0, 0], swapped(w[0, 0])) for w in (w_gate, w_up, w_down)]
@@ -688,12 +694,11 @@
     fa0, fb0, hidden0, recv0, grad_rows = call(
         residual_body, [wide_shape, wide_shape, inner_shape, rows_shape, rows_shape], [arrived, gate0, up0], 4 * flops
     )
-    returned0, grad_rows = lax.optimization_barrier((returned0, grad_rows))
 
     tokens1, send1, weights1 = call(
         middle_body,
         [few, small_shape, ((TOK, EXP), F32)],
-        [tokens0, picks0, weights0, returned0, picks1, gains, routers],
+        [tokens0, mask0, weights0, returned0, mask1, gains, routers],
         600_000_000,
     )
     arrived1 = exchanged(send1)
@@ -717,14 +722,14 @@
         return (kept.astype(F32) + swap.astype(F32)).astype(BF)
 
     args1 = [gate_back1, up_back1, rows1, scaled1, hidden1]
-    sent, kept, sent_near, kept_near = call(grads1_body, [block] * 4, args1, 6 * flops, at)
+    sent, kept, sent_near, kept_near = call(grads1_body, [block] * 4, args1, 6 * flops)
     paired1 = paired_of(kept, swapped(sent))
     got1 = to_owner(paired1, 1)
 
     send2, token_gains = call(
         turn_body,
         [small_shape, ((2, width), F32)],
-        [tokens1, picks1, weights1, returned1, grad1, tokens0, picks0, weights0, returned0, gains, routers],
+        [tokens1, mask1, weights1, returned1, grad1, tokens0, mask0, weights0, returned0, gains, routers],
         900_000_000,
     )
     recv2 = exchanged(send2)
@@ -739,7 +744,6 @@
         [Load(recv2, with_small, 1), Load(fa0, part_rows), Load(fb0, part_rows), down0, recv0, hidden0]
         + [gate0, up0, rows1, gains, token_gains],
         9 * flops,
-        at,
         [pltpu.VMEM((ALL, width), BF), pltpu.VMEM((ALL, inner), BF), pltpu.VMEM((ALL, inner), BF)]
         + [pltpu.VMEM((8, width), F32)],
         order=[(3, 0), (0, 0), (1, 0), (2, 0), (0, 1), (0, 2), (1, 1), (2, 1)] + [(i, 0) for i in range(4, 11)],
@@ -750,20 +754,19 @@
     heard = lax.all_to_all(told, ("dp", "expert"), split_axis=0, concat_axis=0, tiled=True)
     sum0 = paired_of(kept_near, swapped(sent_near))
     high0 = lax.ppermute(sum0, "pipe", [(1, 0)])
-    router_sum, gain_sum = call(heard_body, [((EXP, width), F32), ((1, width), F32)], [heard], 1000)
     thirds = (quarter,) * 3
     final = ((2 * quarter, half), BF)
-    outs = call(
+    *outs, router_sum, gain_sum = call(
         finish_body,
-        [final] * 3,
+        [final] * 3 + [((EXP, width), F32), ((1, width), F32)],
         [
             Either(sum0, low1, thirds),
             Either(high0, sum1, thirds),
             Either(got0[0], got1[0], thirds),
             Either(got0[1], got1[1], thirds),
+            heard,
         ],
         1000,
-        at,
     )
     return (
         outs[0][None, None],

time: 252 us -> 245 us (0.972)
  Pallas kernels: 60 us -> 56 us
  waiting for transfers between devices: 79.3 us -> 76 us
    all_to_all x4, waiting for transfers between devices: 56.7 us -> 52.1 us  [exchanged(): lax.all_to_all(rows, 'expert', split_axis=0, concat_axis=0, tiled=True)]
    pallas_call x11 -> x10, Pallas kernels: 60 us -> 56 us  [call(): pl.pallas_call(kernel, out_shape=out_shape, in_specs=[hbm] * (n + len(oth...]
    select_n x4 -> x3, other arithmetic: 5.1 us -> 8.11 us  [both(): return (jnp.where(first, own, other), jnp.where(first, other, own))]
    all_to_all x4, starting transfers between devices: 26.7 us -> 24.2 us  [exchanged(): lax.all_to_all(rows, 'expert', split_axis=0, concat_axis=0, tiled=True)]
  transfers between devices with their start and end apart: 21 -> 21, of which waited for: 7 -> 9; matrix products, arithmetic and copies ran while one was open for 5% -> 5% of each run, Pallas kernels for 9% -> 8%
where the time goes in v1:
time: 245 us; the launch traced here: 244 us
  waiting for transfers between devices  76 us (31%)
  Pallas kernels  56 us (23%)
  blocking collectives  51 us (21%)
  starting transfers between devices  43 us (18%)
  other arithmetic  13.2 us (5%)
  local copies, waits for them, and re-layouts  3.91 us (2%)
    pallas_call x10, Pallas kernels, call(): pl.pallas_call(kernel, out_shape=out_shape, in_specs=[hbm] * (n + len(oth...  56 us
    all_to_all x4, waiting for transfers between devices, exchanged(): lax.all_to_all(rows, 'expert', split_axis=0, concat_axis=0, tiled=True)  52.1 us
    all_to_all x1, blocking collectives, exchanged(): lax.all_to_all(rows, 'expert', split_axis=0, concat_axis=0, tiled=True)  26.7 us
    all_to_all x1, blocking collectives, shards(): lax.all_to_all(told, ('dp', 'expert'), split_axis=0, concat_axis=0, tiled...  24.3 us
    all_to_all x4, starting transfers between devices, exchanged(): lax.all_to_all(rows, 'expert', split_axis=0, concat_axis=0, tiled=True)  24.2 us
    ppermute x4, waiting for transfers between devices, to_owner(): lax.ppermute(paired, ('dp', 'pipe'), [(2 * d + p, 2 * (1 - d) + owner) fo...  17.6 us
    ppermute x4, starting transfers between devices, to_owner(): lax.ppermute(paired, ('dp', 'pipe'), [(2 * d + p, 2 * (1 - d) + owner) fo...  9.05 us
    select_n x3, other arithmetic, both(): return (jnp.where(first, own, other), jnp.where(first, other, own))  8.11 us
  transfers between devices with their start and end apart: 21, of which 9 were waited for; matrix products, arithmetic and copies ran while one was open for 5% of the time, Pallas kernels for 8%

profile of v1, /device:TPU:0, one launch (start us, length us, event | category | flops | bytes accessed | tf_op | source)
XLA Modules:
  0.0 244.3 jit_solution(9016688492233990527)
XLA Ops:
  3.3 3.6 %shard_map.119 = (bf16[256,5120]{1,0:T(8,128)(2,1)}, f32[64,32]{1,0:T(8,128)}, bf16[64,1024]{1,0:T(8,128)(2,1)}, bf16[64,1024]{1,0:T(8,128)(2,1)}, f32[2,1024]{1...) custom-call(bf16[128,1024]{1,0:T(8,128)(2,1)} %bitcast.46, bf16[128,1024]{1,0:T(8,128)(2,1)} %bitcast.47, ...), custom_call_target="tpu_custom_call" | custom-call | flops 400000000 | bytes 3719168 | tf_op jit(solution)/shard_map/pallas_call | solution.py:334
  6.9 9.8 %all-to-all-start = ((bf16[32,8,5120]{2,1,0:T(8,128)(2,1)}), bf16[32,8,5120]{2,1,0:T(8,128)(2,1)}, u32[]{:S(2)}, u32[]{:S(2)}) async-start(bf16[32,8,5120]{2,1,0:T(8,128)(2,1)} %bitcast.35), calls=%async_computation | async-start | bytes 5242880 | tf_op jit(solution)/shard_map/all_to_all | solution.py:637
  17.4 2.2 collective-permute-done.5
  19.6 2.7 %broadcast_select_fusion = (bf16[512,1024]{1,0:T(8,128)(2,1)}, bf16[512,1024]{1,0:T(8,128)(2,1)}) fusion(bf16[512,1024]{1,0:T(8,128)(2,1)} %collective-permute-done.5, pred[]{:T(512)S(6)} %eq.3, bf16[1,1,512,1024]{3,2,1,0:T(8,128)(2,1)S(1)} %copy-done.2), kind=kLoop, calls=%fused_computation.4 | loop fusion | flops 1048576 | bytes 4194305 | tf_op jit(solution)/shard_map/jit(_where)/select_n | solution.py:653
  22.3 2.7 %broadcast_select_fusion.2 = (bf16[1024,512]{1,0:T(8,128)(2,1)}, bf16[1024,512]{1,0:T(8,128)(2,1)}) fusion(bf16[1024,512]{1,0:T(8,128)(2,1)} %collective-permute-done.4, pred[]{:T(512)S(6)} %eq.3, bf16[1,1,1024,512]{3,2,1,0:T(8,128)(2,1)S(1)} %copy-done.3), kind=kLoop, calls=%fused_computation.6 | loop fusion | flops 1048576 | bytes 4194305 | tf_op jit(solution)/shard_map/jit(_where)/select_n | solution.py:653
  25.0 2.7 %broadcast_select_fusion.4 = (bf16[1024,512]{1,0:T(8,128)(2,1)}, bf16[1024,512]{1,0:T(8,128)(2,1)}) fusion(bf16[1024,512]{1,0:T(8,128)(2,1)} %collective-permute-done.3, pred[]{:T(512)S(6)} %eq.3, bf16[1,1,1024,512]{3,2,1,0:T(8,128)(2,1)S(1)} %copy-done.4), kind=kLoop, calls=%fused_computation.8 | loop fusion | flops 1048576 | bytes 4194305 | tf_op jit(solution)/shard_map/jit(_where)/select_n | solution.py:653
  27.7 25.1 %all-to-all-done = bf16[32,8,5120]{2,1,0:T(8,128)(2,1)} async-done(((bf16[32,8,5120]{2,1,0:T(8,128)(2,1)}), bf16[32,8,5120]{2,1,0:T(8,128)(2,1)}, u32[]{:S(2)}, u32[]{:S(2)}) %all-to-all-start) | async-done | bytes 2621472 | tf_op jit(solution)/shard_map/all_to_all | solution.py:637
  52.8 5.6 %shard_map.120 = bf16[256,2560]{1,0:T(8,128)(2,1)} custom-call(bf16[256,5120]{1,0:T(8,128)(2,1)} %bitcast.9.refs_0_, bf16[1024,512]{1,0:T(8,128)(2,1)} %get-tuple-element.59.refs_1_.refs_6_, bf16[1024,512]{1,0:T(8,128)(2,1)} %get-tuple-element.60.refs_2_.refs_7_, bf16[512,1024]{1,0:T(8,128)(2,1)} %get-tuple-element.61.refs_3_), custom_call_target="tpu_custom_call" | custom-call | flops 2013265920 | bytes 7077888 | tf_op jit(solution)/shard_map/pallas_call | solution.py:334
  58.5 26.7 %all_to_all.61 = bf16[32,8,2560]{2,1,0:T(8,128)(2,1)} all-to-all(bf16[32,8,2560]{2,1,0:T(8,128)(2,1)} %bitcast.39), channel_id=1, replica_groups=mesh['dp'=2,'pipe'=2,'expert'=32] {'expert'}, dimensions={0} | all-to-all | bytes 2621440 | tf_op jit(solution)/shard_map/all_to_all | solution.py:637
  85.2 4.9 %shard_map.121 = (bf16[64,1024]{1,0:T(8,128)(2,1)}, bf16[256,2688]{1,0:T(8,128)(2,1)}, f32[64,32]{1,0:T(8,128)}) custom-call(bf16[64,1024]{1,0:T(8,128)(2,1)} %get-tuple-element.55.refs_0_.refs_5_, f32[64,32]{1,0:T(8,128)} %get-tuple-element.56.refs_1_.refs_6_, f32[64,32]{1,0:T(8,128)} %get-tuple-element.57.refs_2_.refs_7_, bf16[256,2560]{1,0:T(8,128)(2,1)} %bitcast.33, ...), custom_call_target="tpu_custom_call" | custom-call | flops 600000000 | bytes 3121152 | tf_op jit(solution)/shard_map/pallas_call | solution.py:334
  90.2 4.9 %all-to-all-start.2 = ((bf16[32,8,2688]{2,1,0:T(8,128)(2,1)}), bf16[32,8,2688]{2,1,0:T(8,128)(2,1)}, u32[]{:S(2)}, u32[]{:S(2)}) async-start(bf16[32,8,2688]{2,1,0:T(8,128)(2,1)} %bitcast.38), calls=%async_computation.2 | async-start | bytes 2752512 | tf_op jit(solution)/shard_map/all_to_all | solution.py:637
  95.0 5.4 %shard_map.122 = (f32[640,512]{1,0:T(8,128)}, f32[640,512]{1,0:T(8,128)}, bf16[640,512]{1,0:T(8,128)(2,1)}, bf16[640,1024]{1,0:T(8,128)(2,1)}, bf16[640,1024]{1,0:T(8,128)(2,1)}) custom-call(bf16[256,5120]{1,0:T(8,128)(2,1)} %bitcast.9.refs_0_, bf16[1024,512]{1,0:T(8,128)(2,1)} %get-tuple-element.59.refs_1_.refs_6_, ...), custom_call_target="tpu_custom_call" | custom-call | flops 1342177280 | bytes 10616832 | tf_op jit(solution)/shard_map/pallas_call | solution.py:334
  100.5 14.2 %all-to-all-done.2 = bf16[32,8,2688]{2,1,0:T(8,128)(2,1)} async-done(((bf16[32,8,2688]{2,1,0:T(8,128)(2,1)}), bf16[32,8,2688]{2,1,0:T(8,128)(2,1)}, u32[]{:S(2)}, u32[]{:S(2)}) %all-to-all-start.2) | async-done | bytes 1376288 | tf_op jit(solution)/shard_map/all_to_all | solution.py:637
  114.6 9.3 %shard_map.123 = (bf16[256,2688]{1,0:T(8,128)(2,1)}, bf16[640,1024]{1,0:T(8,128)(2,1)}, bf16[640,1024]{1,0:T(8,128)(2,1)}, bf16[640,512]{1,0:T(8,128)(2,1)}, bf1...) custom-call(bf16[256,2688]{1,0:T(8,128)(2,1)} %bitcast.16.refs_0_, bf16[640,1024]{1,0:T(8,128)(2,1)} %get-tuple-element.68.refs_1_, ...), custom_call_target="tpu_custom_call" | custom-call | flops 4026531840 | bytes 11796480 | tf_op jit(solution)/shard_map/pallas_call | solution.py:334
  124.0 4.7 %all-to-all-start.3 = ((bf16[32,8,2688]{2,1,0:T(8,128)(2,1)}), bf16[32,8,2688]{2,1,0:T(8,128)(2,1)}, u32[]{:S(2)}, u32[]{:S(2)}) async-start(bf16[32,8,2688]{2,1,0:T(8,128)(2,1)} %bitcast.37), calls=%async_computation.3 | async-start | bytes 2752512 | tf_op jit(solution)/shard_map/all_to_all | solution.py:637
  128.7 5.9 %shard_map.125 = (bf16[768,512]{1,0:T(8,128)(2,1)}, bf16[768,512]{1,0:T(8,128)(2,1)}, bf16[768,512]{1,0:T(8,128)(2,1)}, bf16[768,512]{1,0:T(8,128)(2,1)}) custom-call(bf16[640,512]{1,0:T(8,128)(2,1)} %get-tuple-element.75.refs_0_, bf16[640,512]{1,0:T(8,128)(2,1)} %get-tuple-element.76.refs_1_, bf16[640,1024]{1,0:T(8,128)(2,1)} %get-tuple-element.77.refs_2_.refs_8_, ...), custom_call_target="tpu_custom_call" | custom-call | flops 2013265920 | bytes 7733248 | tf_op jit(solution)/shard_map/pallas_call | solution.py:334
  135.2 12.8 %all-to-all-done.3 = bf16[32,8,2688]{2,1,0:T(8,128)(2,1)} async-done(((bf16[32,8,2688]{2,1,0:T(8,128)(2,1)}), bf16[32,8,2688]{2,1,0:T(8,128)(2,1)}, u32[]{:S(2)}, u32[]{:S(2)}) %all-to-all-start.3) | async-done | bytes 1376288 | tf_op jit(solution)/shard_map/all_to_all | solution.py:637
  148.0 6.7 %shard_map.124 = (bf16[256,2688]{1,0:T(8,128)(2,1)}, f32[2,1024]{1,0:T(2,128)}) custom-call(bf16[64,1024]{1,0:T(8,128)(2,1)} %get-tuple-element.65.refs_0_, f32[64,32]{1,0:T(8,128)} %get-tuple-element.62.refs_4_.refs_1_, f32[64,32]{1,0:T(8,128)} %get-tuple-element.66.refs_2_, bf16[256,2688]{1,0:T(8,128)(2,1)} %bitcast.18.refs_3_, ...), custom_call_target="tpu_custom_call" | custom-call | flops 900000000 | bytes 4636672 | tf_op jit(solution)/shard_map/pallas_call | solution.py:334
  154.7 4.8 %all-to-all-start.4 = ((bf16[32,8,2688]{2,1,0:T(8,128)(2,1)}), bf16[32,8,2688]{2,1,0:T(8,128)(2,1)}, u32[]{:S(2)}, u32[]{:S(2)}) async-start(bf16[32,8,2688]{2,1,0:T(8,128)(2,1)} %bitcast.36), calls=%async_computation.4 | async-start | bytes 2752512 | tf_op jit(solution)/shard_map/all_to_all | solution.py:637
  160.5 1.3 add_convert_fusion.3.refs_6_
  163.2 1.3 add_convert_fusion.2
  165.3 4.4 %collective-permute-start.9 = (bf16[768,512]{1,0:T(8,128)(2,1)S(1)}, bf16[768,512]{1,0:T(8,128)(2,1)}, u32[]{:S(2)}, u32[]{:S(2)}) collective-permute-start(bf16[768,512]{1,0:T(8,128)(2,1)S(1)} %add_convert_fusion.2), channel_id=1, source_target_pairs={{0,96},{64,32},{1,97},{65,33},{2,98},{66,34},{3,99},{67,35},{4,100... | collective-permute-start | bytes 2359304 | tf_op jit(solution)/shard_map/ppermute | solution.py:718
  171.4 17.6 %collective-permute-done.9.refs_7_ = bf16[768,512]{1,0:T(8,128)(2,1)} collective-permute-done((bf16[768,512]{1,0:T(8,128)(2,1)S(1)}, bf16[768,512]{1,0:T(8,128)(2,1)}, u32[]{:S(2)}, u32[]{:S(2)}) %collective-permute-start.9) | collective-permute-done | bytes 786464 | tf_op jit(solution)/shard_map/ppermute | solution.py:718
  189.0 8.8 %shard_map.126 = (bf16[768,512]{1,0:T(8,128)(2,1)}, bf16[768,512]{1,0:T(8,128)(2,1)}, bf16[768,512]{1,0:T(8,128)(2,1)}, bf16[768,512]{1,0:T(8,128)(2,1)}, f32[2,1024]{1,0:T(2,128)}, /*index=5*/f32[2,1024]{1,0:T(2,128)}) custom-call(bf16[256,2688]{1,0:T(8,128)(2,1)} %bitcast.20.refs_0_, f32[640,512]{1,0:T(8,128)} %get-tuple-element.85.refs_1_, ...), custom_call_target="tpu_custom_call" | custom-call | flops 3019898880 | bytes 13598720 | tf_op jit(solution)/shard_map/pallas_call | solution.py:334
  197.8 3.2 %collective-permute-start.11 = (bf16[768,512]{1,0:T(8,128)(2,1)}, bf16[768,512]{1,0:T(8,128)(2,1)S(1)}, u32[]{:S(2)}, u32[]{:S(2)}) collective-permute-start(bf16[768,512]{1,0:T(8,128)(2,1)} %get-tuple-element.91), channel_id=1, source_target_pairs={{0,32},{32,0},{1,33},{33,1},{2,34},{34,2},{3,35},{35,3},{4,36},{36... | collective-permute-start | bytes 2359304 | tf_op jit(solution)/shard_map/ppermute | solution.py:641
  201.1 2.0 collective-permute-done.11
  204.5 1.4 collective-permute-start.12
  208.3 2.7 %collective-permute-start.14 = (bf16[768,512]{1,0:T(8,128)(2,1)}, bf16[768,512]{1,0:T(8,128)(2,1)}, u32[]{:S(2)}, u32[]{:S(2)}) collective-permute-start(bf16[768,512]{1,0:T(8,128)(2,1)} %add_convert_fusion), channel_id=1, source_target_pairs={{0,64},{64,0},{1,65},{65,1},{2,66},{66,2},{3,67},{67,3},{4,68},{68... | collective-permute-start | bytes 2359304 | tf_op jit(solution)/shard_map/ppermute | solution.py:718
  211.0 1.8 collective-permute-start.16
  214.2 1.9 shard_map.127
  216.1 24.3 %all_to_all.62.refs_4_ = f32[64,16,128]{2,1,0:T(8,128)} all-to-all(f32[64,16,128]{2,1,0:T(8,128)} %shard_map.127), channel_id=1, replica_groups=mesh['dp'=2,'pipe'=2,'expert'=32] {'dp','expert'}, dimensions={0} | all-to-all | bytes 1048576 | tf_op jit(solution)/shard_map/all_to_all | solution.py:754
  240.4 3.7 %shard_map.128 = (bf16[512,512]{1,0:T(8,128)(2,1)}, bf16[512,512]{1,0:T(8,128)(2,1)}, bf16[512,512]{1,0:T(8,128)(2,1)}, f32[32,1024]{1,0:T(8,128)}, f32[1,1024]{1,0:T(1,128)}) custom-call(bf16[768,512]{1,0:T(8,128)(2,1)} %copy-done.1, bf16[768,512]{1,0:T(8,128)(2,1)} %collective-permute-done.12.refs_1_, bf16[768,512]{1,0:T(8,128)(2,1)} %collective-permute-done.14.refs_2_, ...), custom_call_target="tpu_custom_call" | custom-call | flops 1000 | bytes 5378048 | tf_op jit(solution)/shard_map/pallas_call | solution.py:334
  (61 shorter events, 13.9 us)
Async XLA Ops:
  0.6 2.0 collective-permute-start.2
  0.7 1.5 collective-permute-start.1
  1.2 1.4 collective-permute-start
  6.9 9.8 %copy-start.2 = (bf16[1,1,512,1024]{3,2,1,0:T(8,128)(2,1)S(1)}, bf16[1,1,512,1024]{3,2,1,0:T(8,128)(2,1)}, u32[]{:S(2)}) copy-start(bf16[1,1,512,1024]{3,2,1,0:T(8,128)(2,1)} %param.14) | copy-start | bytes 3145732
  6.9 9.9 %copy-start.3 = (bf16[1,1,1024,512]{3,2,1,0:T(8,128)(2,1)S(1)}, bf16[1,1,1024,512]{3,2,1,0:T(8,128)(2,1)}, u32[]{:S(2)}) copy-start(bf16[1,1,1024,512]{3,2,1,0:T(8,128)(2,1)} %param.13) | copy-start | bytes 3145732
  6.9 10.4 %copy-start.4 = (bf16[1,1,1024,512]{3,2,1,0:T(8,128)(2,1)S(1)}, bf16[1,1,1024,512]{3,2,1,0:T(8,128)(2,1)}, u32[]{:S(2)}) copy-start(bf16[1,1,1024,512]{3,2,1,0:T(8,128)(2,1)} %param.12) | copy-start | bytes 3145732
  6.9 45.9 %all-to-all-start = ((bf16[32,8,5120]{2,1,0:T(8,128)(2,1)}), bf16[32,8,5120]{2,1,0:T(8,128)(2,1)}, u32[]{:S(2)}, u32[]{:S(2)}) async-start(bf16[32,8,5120]{2,1,0:T(8,128)(2,1)} %bitcast.35), calls=%async_computation | async-start | bytes 5242880 | tf_op jit(solution)/shard_map/all_to_all | solution.py:637
  16.7 2.9 %collective-permute-start.5 = (bf16[512,1024]{1,0:T(8,128)(2,1)S(1)}, bf16[512,1024]{1,0:T(8,128)(2,1)}, u32[]{:S(2)}, u32[]{:S(2)}) collective-permute-start(bf16[512,1024]{1,0:T(8,128)(2,1)S(1)} %bitcast.40), channel_id=1, source_target_pairs={{0,32},{32,0},{1,33},{33,1},{2,34},{34,2},{3,35},{35,3},{4,36},{36... | collective-permute-start | bytes 3145736 | tf_op jit(solution)/shard_map/ppermute | solution.py:641
  16.8 5.5 %collective-permute-start.4 = (bf16[1024,512]{1,0:T(8,128)(2,1)S(1)}, bf16[1024,512]{1,0:T(8,128)(2,1)}, u32[]{:S(2)}, u32[]{:S(2)}) collective-permute-start(bf16[1024,512]{1,0:T(8,128)(2,1)S(1)} %bitcast.41), channel_id=1, source_target_pairs={{0,32},{32,0},{1,33},{33,1},{2,34},{34,2},{3,35},{35,3},{4,36},{36... | collective-permute-start | bytes 3145736 | tf_op jit(solution)/shard_map/ppermute | solution.py:641
  17.3 7.7 %collective-permute-start.3 = (bf16[1024,512]{1,0:T(8,128)(2,1)S(1)}, bf16[1024,512]{1,0:T(8,128)(2,1)}, u32[]{:S(2)}, u32[]{:S(2)}) collective-permute-start(bf16[1024,512]{1,0:T(8,128)(2,1)S(1)} %bitcast.42), channel_id=1, source_target_pairs={{0,32},{32,0},{1,33},{33,1},{2,34},{34,2},{3,35},{35,3},{4,36},{36... | collective-permute-start | bytes 3145736 | tf_op jit(solution)/shard_map/ppermute | solution.py:641
  90.2 24.5 %all-to-all-start.2 = ((bf16[32,8,2688]{2,1,0:T(8,128)(2,1)}), bf16[32,8,2688]{2,1,0:T(8,128)(2,1)}, u32[]{:S(2)}, u32[]{:S(2)}) async-start(bf16[32,8,2688]{2,1,0:T(8,128)(2,1)} %bitcast.38), calls=%async_computation.2 | async-start | bytes 2752512 | tf_op jit(solution)/shard_map/all_to_all | solution.py:637
  124.0 24.0 %all-to-all-start.3 = ((bf16[32,8,2688]{2,1,0:T(8,128)(2,1)}), bf16[32,8,2688]{2,1,0:T(8,128)(2,1)}, u32[]{:S(2)}, u32[]{:S(2)}) async-start(bf16[32,8,2688]{2,1,0:T(8,128)(2,1)} %bitcast.37), calls=%async_computation.3 | async-start | bytes 2752512 | tf_op jit(solution)/shard_map/all_to_all | solution.py:637
  134.6 25.0 %collective-permute-start.6 = (bf16[768,512]{1,0:T(8,128)(2,1)}, bf16[768,512]{1,0:T(8,128)(2,1)S(1)}, u32[]{:S(2)}, u32[]{:S(2)}) collective-permute-start(bf16[768,512]{1,0:T(8,128)(2,1)} %get-tuple-element.81), channel_id=1, source_target_pairs={{0,32},{32,0},{1,33},{33,1},{2,34},{34,2},{3,35},{35,3},{4,36},{36... | collective-permute-start | bytes 2359304 | tf_op jit(solution)/shard_map/ppermute | solution.py:641
  134.7 28.5 %collective-permute-start.8 = (bf16[768,512]{1,0:T(8,128)(2,1)}, bf16[768,512]{1,0:T(8,128)(2,1)}, u32[]{:S(2)}, u32[]{:S(2)}) collective-permute-start(bf16[768,512]{1,0:T(8,128)(2,1)} %get-tuple-element.83), channel_id=1, source_target_pairs={{0,32},{32,0},{1,33},{33,1},{2,34},{34,2},{3,35},{35,3},{4,36},{36... | collective-permute-start | bytes 2359304 | tf_op jit(solution)/shard_map/ppermute | solution.py:641
  154.7 5.8 %copy-start.6 = (bf16[768,512]{1,0:T(8,128)(2,1)S(1)}, bf16[768,512]{1,0:T(8,128)(2,1)}, u32[]{:S(2)}) copy-start(bf16[768,512]{1,0:T(8,128)(2,1)} %get-tuple-element.80) | copy-start | bytes 2359300
  154.7 34.2 %all-to-all-start.4 = ((bf16[32,8,2688]{2,1,0:T(8,128)(2,1)}), bf16[32,8,2688]{2,1,0:T(8,128)(2,1)}, u32[]{:S(2)}, u32[]{:S(2)}) async-start(bf16[32,8,2688]{2,1,0:T(8,128)(2,1)} %bitcast.36), calls=%async_computation.4 | async-start | bytes 2752512 | tf_op jit(solution)/shard_map/all_to_all | solution.py:637
  159.6 3.6 %copy-start.5 = (bf16[768,512]{1,0:T(8,128)(2,1)S(1)}, bf16[768,512]{1,0:T(8,128)(2,1)}, u32[]{:S(2)}) copy-start(bf16[768,512]{1,0:T(8,128)(2,1)} %get-tuple-element.82) | copy-start | bytes 2359300
  159.6 0.9 copy-start.8
  161.8 36.0 %copy-start = (bf16[768,512]{1,0:T(8,128)(2,1)}, bf16[768,512]{1,0:T(8,128)(2,1)S(1)}, u32[]{:S(2)}) copy-start(bf16[768,512]{1,0:T(8,128)(2,1)S(1)} %add_convert_fusion.3.refs_6_) | copy-start | bytes 2359300
  161.8 7.8 %collective-permute-start.7 = (bf16[768,512]{1,0:T(8,128)(2,1)S(1)}, bf16[768,512]{1,0:T(8,128)(2,1)S(1)}, u32[]{:S(2)}, u32[]{:S(2)}) collective-permute-start(bf16[768,512]{1,0:T(8,128)(2,1)S(1)} %add_convert_fusion.3.refs_6_), channel_id=1, source_target_pairs={{0,32},{1,33},{2,34},{3,35},{4,36},{5,37},{6,38},{7,39},{8,40},{9,... | collective-permute-start | bytes 2359304 | tf_op jit(solution)/shard_map/ppermute | solution.py:737
  164.5 5.1 %collective-permute-start.10 = (bf16[768,512]{1,0:T(8,128)(2,1)S(1)}, bf16[768,512]{1,0:T(8,128)(2,1)S(1)}, u32[]{:S(2)}, u32[]{:S(2)}) collective-permute-start(bf16[768,512]{1,0:T(8,128)(2,1)S(1)} %add_convert_fusion.2), channel_id=1, source_target_pairs={{32,96},{96,32},{33,97},{97,33},{34,98},{98,34},{35,99},{99,35},{3... | collective-permute-start | bytes 2359304 | tf_op jit(solution)/shard_map/ppermute | solution.py:718
  165.3 23.7 %collective-permute-start.9 = (bf16[768,512]{1,0:T(8,128)(2,1)S(1)}, bf16[768,512]{1,0:T(8,128)(2,1)}, u32[]{:S(2)}, u32[]{:S(2)}) collective-permute-start(bf16[768,512]{1,0:T(8,128)(2,1)S(1)} %add_convert_fusion.2), channel_id=1, source_target_pairs={{0,96},{64,32},{1,97},{65,33},{2,98},{66,34},{3,99},{67,35},{4,100... | collective-permute-start | bytes 2359304 | tf_op jit(solution)/shard_map/ppermute | solution.py:718
  170.5 0.9 copy-start.10
  197.8 8.1 %copy-start.7 = (bf16[768,512]{1,0:T(8,128)(2,1)S(1)}, bf16[768,512]{1,0:T(8,128)(2,1)}, u32[]{:S(2)}) copy-start(bf16[768,512]{1,0:T(8,128)(2,1)} %get-tuple-element.92) | copy-start | bytes 2359300
  197.8 5.3 %collective-permute-start.11 = (bf16[768,512]{1,0:T(8,128)(2,1)}, bf16[768,512]{1,0:T(8,128)(2,1)S(1)}, u32[]{:S(2)}, u32[]{:S(2)}) collective-permute-start(bf16[768,512]{1,0:T(8,128)(2,1)} %get-tuple-element.91), channel_id=1, source_target_pairs={{0,32},{32,0},{1,33},{33,1},{2,34},{34,2},{3,35},{35,3},{4,36},{36... | collective-permute-start | bytes 2359304 | tf_op jit(solution)/shard_map/ppermute | solution.py:641
  201.0 4.9 %collective-permute-start.13 = (bf16[768,512]{1,0:T(8,128)(2,1)}, bf16[768,512]{1,0:T(8,128)(2,1)S(1)}, u32[]{:S(2)}, u32[]{:S(2)}) collective-permute-start(bf16[768,512]{1,0:T(8,128)(2,1)} %get-tuple-element.93), channel_id=1, source_target_pairs={{0,32},{32,0},{1,33},{33,1},{2,34},{34,2},{3,35},{35,3},{4,36},{36... | collective-permute-start | bytes 2359304 | tf_op jit(solution)/shard_map/ppermute | solution.py:641
  204.5 35.9 %copy-start.1 = (bf16[768,512]{1,0:T(8,128)(2,1)}, bf16[768,512]{1,0:T(8,128)(2,1)S(1)}, u32[]{:S(2)}) copy-start(bf16[768,512]{1,0:T(8,128)(2,1)S(1)} %add_convert_fusion.1.refs_0_) | copy-start | bytes 2359300
  204.5 6.5 %copy-start.14 = (f32[2,1024]{1,0:T(2,128)S(1)}, f32[2,1024]{1,0:T(2,128)}, u32[]{:S(2)}) copy-start(f32[2,1024]{1,0:T(2,128)} %get-tuple-element.95) | copy-start | bytes 24580
  204.5 35.9 %collective-permute-start.12 = (bf16[768,512]{1,0:T(8,128)(2,1)S(1)}, bf16[768,512]{1,0:T(8,128)(2,1)}, u32[]{:S(2)}, u32[]{:S(2)}) collective-permute-start(bf16[768,512]{1,0:T(8,128)(2,1)S(1)} %add_convert_fusion.1.refs_0_), channel_id=1, source_target_pairs={{32,0},{33,1},{34,2},{35,3},{36,4},{37,5},{38,6},{39,7},{40,8},{41... | collective-permute-start | bytes 2359304 | tf_op jit(solution)/shard_map/ppermute | solution.py:756
  207.0 33.3 %collective-permute-start.15 = (bf16[768,512]{1,0:T(8,128)(2,1)}, bf16[768,512]{1,0:T(8,128)(2,1)}, u32[]{:S(2)}, u32[]{:S(2)}) collective-permute-start(bf16[768,512]{1,0:T(8,128)(2,1)} %add_convert_fusion), channel_id=1, source_target_pairs={{32,64},{96,0},{33,65},{97,1},{34,66},{98,2},{35,67},{99,3},{36,68... | collective-permute-start | bytes 2359304 | tf_op jit(solution)/shard_map/ppermute | solution.py:718
  208.3 32.0 %collective-permute-start.14 = (bf16[768,512]{1,0:T(8,128)(2,1)}, bf16[768,512]{1,0:T(8,128)(2,1)}, u32[]{:S(2)}, u32[]{:S(2)}) collective-permute-start(bf16[768,512]{1,0:T(8,128)(2,1)} %add_convert_fusion), channel_id=1, source_target_pairs={{0,64},{64,0},{1,65},{65,1},{2,66},{66,2},{3,67},{67,3},{4,68},{68... | collective-permute-start | bytes 2359304 | tf_op jit(solution)/shard_map/ppermute | solution.py:718
  211.0 2.6 %collective-permute-start.16 = (f32[2,1024]{1,0:T(2,128)S(1)}, f32[2,1024]{1,0:T(2,128)S(1)}, u32[]{:S(2)}, u32[]{:S(2)}) collective-permute-start(f32[2,1024]{1,0:T(2,128)S(1)} %copy-done.14), channel_id=1, source_target_pairs={{0,32},{32,0},{1,33},{33,1},{2,34},{34,2},{3,35},{35,3},{4,36},{36... | collective-permute-start | bytes 24584 | tf_op jit(solution)/shard_map/ppermute | solution.py:641
  (5 other events, 3.3 us)
